TPU v7x, 32 devices: a whole 2x2x4 slice. The times are simulated.
32 devices in a mesh: section: 4 (over y, x), coil: 4 (over z), cuts: 2 (over core).
Axes of the slice: x: 2, y: 2, z: 4, core: 2. Of those that a mesh axis runs over, the one named last changes fastest.
Arguments:
- initial: bfloat16 [2, 32, 80, 2, 128], P(None, 'coil', 'cuts'), may hold values from -6 to 6
- sens: bfloat16 [2, 8, 32, 80, 2, 128], P(None, ('coil', 'cuts')), may hold values from -2.5 to 2.5
- kspace: bfloat16 [2, 8, 32, 80, 2, 128], P(None, ('coil', 'cuts')), may hold values from -6 to 6
- mask: int32 [2, 80, 128], replicated, may hold values 0 or 1
- step_sizes: float32 [4], P('section'), may hold values from 0.3 to 1.5
- conv_in: bfloat16 [4, 128, 18], P('section'), may hold values from -1.5 to 1.5
- bias_in: float32 [4, 128], P('section'), may hold values from -3 to 3
- conv_out: bfloat16 [4, 18, 128], P('section'), may hold values from -0.1875 to 0.1875
Outputs:
- cascade_images: bfloat16 [4, 2, 32, 80, 2, 128], P('section', None, 'coil', 'cuts')
Inputs may be any that keep to these rules, and one draw needn't show every extreme that they name: `mask`: 1 marks a sampled phase-encoding line of the slab, 0 one that was not measured.
All inputs are finite; a program needn't handle non-finite values.
Results may differ from a plain program's by a relative error of at most 0.028.
Values may be sent and summed in bfloat16 or wider, within the bound.
No kernel may reach another device: no remote copies, remote signals or barrier semaphores. Data moves between devices by JAX's collectives and lax.ppermute only.
A program may use at most 128 MiB of HBM per device.

v0:
```python
import math
import jax
import jax.numpy as jnp
from jax import lax
from jax.sharding import PartitionSpec as P


def extended_2(x, sides, width):
    for axis, dim in sides:
        size, length = (lax.axis_size(axis), x.shape[dim])
        up = [(i, (i + 1) % size) for i in range(size - 1)]
        down = [(j, i) for i, j in up]
        last = lax.slice_in_dim(x, length - width, length, axis=dim)
        leading = lax.slice_in_dim(x, 0, width, axis=dim)
        before = lax.ppermute(last, axis, up)
        after = lax.ppermute(leading, axis, down)
        x = jnp.concatenate([before, x, after], axis=dim)
    return x


def from_partner(block, axis, bit):
    count = lax.axis_size(axis)
    route = []
    for low in range(count):
        high = low | 1 << bit
        if high != low and high < count:
            route += [(low, high), (high, low)]
    return lax.ppermute(block, axis, route)


def dft_table(length, sign):
    ramp = jnp.arange(length, dtype=jnp.int32)
    phase = ramp[:, None] * ramp[None, :] % length
    angle = phase.astype(jnp.float32) * (2.0 * math.pi / length)
    scale = 1.0 / math.sqrt(length)
    cosine = jnp.cos(angle) * scale
    sine = jnp.sin(angle) * (scale * sign)
    upper = jnp.concatenate([cosine, -sine], axis=1)
    lower = jnp.concatenate([sine, cosine], axis=1)
    return jnp.concatenate([upper, lower], axis=0).astype(jnp.bfloat16)


def pass_last(volume, table):
    shape = volume.shape
    flat = volume.reshape(-1, shape[-2] * shape[-1])
    return (
        jnp.dot(flat, table, preferred_element_type=jnp.float32).astype(jnp.bfloat16).reshape(shape)
    )


def pass_middle(volume, table):
    length = volume.shape[1]
    split = table.reshape(2, length, 2, length)
    return jnp.einsum("pjcz,cjdk->pkdz", volume, split, preferred_element_type=jnp.float32).astype(
        jnp.bfloat16
    )


def pass_first(volume, table):
    length = volume.shape[0]
    split = table.reshape(2, length, 2, length)
    return jnp.einsum("jycz,cjdk->kydz", volume, split, preferred_element_type=jnp.float32).astype(
        jnp.bfloat16
    )


def complex_product(sens, image):
    sens_real = sens[:, :, 0].astype(jnp.float32)
    sens_imag = sens[:, :, 1].astype(jnp.float32)
    image_real = image[:, :, 0].astype(jnp.float32)
    image_imag = image[:, :, 1].astype(jnp.float32)
    return jnp.stack(
        [
            sens_real * image_real - sens_imag * image_imag,
            sens_real * image_imag + sens_imag * image_real,
        ],
        axis=2,
    )


def conj_product(sens, back):
    sens_real = sens[:, :, 0].astype(jnp.float32)
    sens_imag = sens[:, :, 1].astype(jnp.float32)
    back_real = back[:, :, 0].astype(jnp.float32)
    back_imag = back[:, :, 1].astype(jnp.float32)
    return jnp.stack(
        [
            sens_real * back_real + sens_imag * back_imag,
            sens_real * back_imag - sens_imag * back_real,
        ],
        axis=2,
    )


def hidden_layer(extended, out_rows, weights_in, bias):
    width = extended.shape[3]
    padded = jnp.pad(extended, ((0, 0), (0, 0), (0, 0), (1, 1)))
    taps = jnp.stack(
        [
            padded[:, shift_row : shift_row + out_rows, :, shift_col : shift_col + width]
            for shift_row in range(3)
            for shift_col in range(3)
        ],
        axis=2,
    )
    taps = taps.reshape(extended.shape[0], out_rows, 18, width)
    summed = jnp.einsum("hf,xyfz->xyhz", weights_in, taps, preferred_element_type=jnp.float32)
    return jax.nn.silu(summed + bias[None, None, :, None]).astype(jnp.bfloat16)


def combine_taps(beside_all, rows):
    width = beside_all.shape[3]
    padded = jnp.pad(beside_all, ((0, 0), (0, 0), (0, 0), (1, 1)))
    total = jnp.zeros((beside_all.shape[0], rows, 2, width), jnp.float32)
    for shift_row in range(3):
        for shift_col in range(3):
            first = (3 * shift_row + shift_col) * 2
            total = (
                total
                + padded[
                    :,
                    shift_row : shift_row + rows,
                    first : first + 2,
                    shift_col : shift_col + width,
                ]
            )
    return total


def refine_rows(current, weights_in, bias, weights_out):
    rows = current.shape[1]
    extended = extended_2(current, (("cuts", 1),), 1)
    hidden = hidden_layer(extended, rows, weights_in, bias)
    product = jnp.einsum("fh,xyhz->xyfz", weights_out, hidden, preferred_element_type=jnp.float32)
    beside_all = extended_2(product.astype(jnp.bfloat16), (("cuts", 1),), 1).astype(product.dtype)
    return combine_taps(beside_all, rows)


def whole_rows(current):
    return lax.all_gather(current, "cuts", axis=1, tiled=True)


def sum_gradient(back_rows, current):
    mine = lax.psum_scatter(
        back_rows(jnp.int32(0), lax.axis_size("coil") * current.shape[0]).astype(jnp.bfloat16),
        "coil",
        scatter_dimension=0,
        tiled=True,
    )
    grad = lax.psum_scatter(mine, "cuts", scatter_dimension=1, tiled=True).astype(jnp.float32)
    return grad


def finish_step(current, grad, step, weights_in, bias, weights_out):
    refine = refine_rows(current, weights_in, bias, weights_out)
    return (current.astype(jnp.float32) - step * grad + refine).astype(jnp.bfloat16)


def pair_block(current, sens_one, data_one, mask_one, step, weights_in, bias, weights_out, half):
    halves = whole_rows(current)
    whole = lax.all_gather(halves, "coil", axis=0, tiled=True)
    size_x, size_y, _, size_z = whole.shape
    half_x = size_x // 2
    half_y = size_y // 2
    forward_x, forward_y, forward_z = (
        dft_table(size_x, 1.0),
        dft_table(size_y, 1.0),
        dft_table(size_z, 1.0),
    )
    back_x, back_y, back_z = (
        dft_table(size_x, -1.0),
        dft_table(size_y, -1.0),
        dft_table(size_z, -1.0),
    )
    lower_side = half == 0
    x_start = half * half_x
    x_other = (1 - half) * half_x
    y_start = half * half_y
    y_other = (1 - half) * half_y
    rows_in = lax.dynamic_slice_in_dim(whole, x_start, half_x, 0)
    sens_rows = lax.dynamic_slice_in_dim(sens_one, x_start, half_x, 0)
    coil_image = complex_product(sens_rows, rows_in).astype(jnp.bfloat16)
    partial_value = pass_middle(pass_last(coil_image, forward_z), forward_y)
    kept = lax.dynamic_slice_in_dim(partial_value, y_start, half_y, 1)
    sent = lax.dynamic_slice_in_dim(partial_value, y_other, half_y, 1)
    arrived = from_partner(sent, "section", 0)
    assembled = jnp.concatenate(
        [jnp.where(lower_side, kept, arrived), jnp.where(lower_side, arrived, kept)], axis=0
    )
    predicted = pass_first(assembled, forward_x)
    data_half = lax.dynamic_slice_in_dim(data_one, y_start, half_y, 1)
    mask_half = lax.dynamic_slice_in_dim(mask_one, y_start, half_y, 0)
    weight_mask = mask_half.astype(jnp.float32)[None, :, None, :]
    resid = (weight_mask * (data_half.astype(jnp.float32) - predicted.astype(jnp.float32))).astype(
        jnp.bfloat16
    )
    spectrum = pass_first(resid, back_x)
    kept_back = lax.dynamic_slice_in_dim(spectrum, x_start, half_x, 0)
    sent_back = lax.dynamic_slice_in_dim(spectrum, x_other, half_x, 0)
    arrived_back = from_partner(sent_back, "section", 0)
    joined = jnp.concatenate(
        [
            jnp.where(lower_side, kept_back, arrived_back),
            jnp.where(lower_side, arrived_back, kept_back),
        ],
        axis=1,
    )
    back = pass_last(pass_middle(joined, back_y), back_z)
    term = conj_product(sens_rows, back)
    blank = jnp.zeros_like(term)
    full_term = jnp.concatenate(
        [jnp.where(lower_side, term, blank), jnp.where(lower_side, blank, term)], axis=0
    )

    def back_rows(start, count):
        return full_term

    grad = sum_gradient(back_rows, current)
    grad = grad + from_partner(grad.astype(jnp.bfloat16), "section", 0).astype(grad.dtype)
    return finish_step(current, grad, step, weights_in, bias, weights_out)


def body(initial, sens, kspace, mask, step_sizes, conv_in, bias_in, conv_out):
    section_count = lax.axis_size("section")
    position = lax.axis_index("section")
    all_steps, all_bias = (
        lax.all_gather(step_sizes, "section", axis=0, tiled=True),
        lax.all_gather(bias_in, "section", axis=0, tiled=True),
    )
    all_in, all_out = (
        lax.all_gather(conv_in, "section", axis=0, tiled=True),
        lax.all_gather(conv_out, "section", axis=0, tiled=True),
    )
    slab = position // 2
    half = position % 2
    current = lax.dynamic_index_in_dim(initial, slab, 0, keepdims=False)
    sens_one = lax.dynamic_index_in_dim(sens, slab, 0, keepdims=False)[0]
    data_one = lax.dynamic_index_in_dim(kspace, slab, 0, keepdims=False)[0]
    mask_one = lax.dynamic_index_in_dim(mask, slab, 0, keepdims=False)
    images = []
    for cascade in range(section_count):
        current = pair_block(
            current,
            sens_one,
            data_one,
            mask_one,
            all_steps[cascade],
            all_in[cascade],
            all_bias[cascade],
            all_out[cascade],
            half,
        )
        images.append(current)
    stacked = jnp.stack(images, axis=0)[:, None]
    arrived = lax.all_to_all(stacked, "section", split_axis=0, concat_axis=1, tiled=True)
    return arrived[:, ::2]


def solution(mesh):
    return jax.shard_map(
        body,
        mesh=mesh,
        in_specs=(
            P(None, "coil", "cuts", None, None),
            P(None, ("coil", "cuts"), None, None, None, None),
            P(None, ("coil", "cuts"), None, None, None, None),
            P(),
            P("section"),
            P("section", None, None),
            P("section", None),
            P("section", None, None),
        ),
        out_specs=P("section", None, "coil", "cuts", None, None),
        check_vma=False,
    )
```

profile of v0, /device:TPU:0, one launch (start us, length us, event | category | flops | bytes accessed | tf_op | source)
XLA Modules:
  0.0 516.5 jit_solution(3672511079097253560)
XLA Ops:
  7.8 2.3 all-gather
  12.5 32.9 %all-gather.14.cloned.1.call-done = bf16[1,32,80,2,128]{4,2,3,0,1:T(8,128)(2,1)} async-done(((bf16[1,8,80,2,128]{4,2,3,0,1:T(8,128)(2,1)}), bf16[1,32,80,2,128]{4,2,3,0,1:T(8,128)(2,1)}) %all-gather.14.cloned.1.call-update) | async-done | bytes 1310736 | tf_op jit(solution)/shard_map/all_gather | solution.py:161
  48.3 1.5 collective-permute-start
  51.0 1.6 constant_dynamic-slice_fusion
  52.6 4.5 collective-permute-done
  58.4 1.6 collective-permute-start.1
  60.5 5.9 %collective-permute-done.1 = bf16[16,40,2,128]{3,1,0,2:T(8,128)(2,1)S(1)} collective-permute-done((bf16[16,40,2,128]{3,1,0,2:T(8,128)(2,1)S(1)}, bf16[16,40,2,128]{3,1,0,2:T(8,128)(2,1)S(1)}, u32[]{:S(2)}, u32[]{:S(2)}) %collective-permute-start.1) | collective-permute-done | bytes 327712 | tf_op jit(solution)/shard_map/ppermute | solution.py:28
  75.5 7.9 %all-gather.2 = f32[4,1,128]{2,1,0:T(1,128)S(1)} all-gather(f32[1,1,128]{2,1,0:T(1,128)S(1)} %bitcast.665), channel_id=1, replica_groups=mesh['section'=4,'coil'=4,'cuts'=2] {'section'}, dimensions={0}, use_global_device_ids=true | all-gather | bytes 2560 | tf_op jit(solution)/shard_map/all_gather | solution.py:228
  83.4 8.1 %all_gather.39 = bf16[4,128,18]{1,2,0:T(8,128)(2,1)S(1)} all-gather(bf16[1,128,18]{1,2,0:T(8,128)(2,1)S(1)} %copy-done.37), channel_id=1, replica_groups=mesh['section'=4,'coil'=4,'cuts'=2] {'section'}, dimensions={0}, use_global_device_ids=true | all-gather | bytes 23040 | tf_op jit(solution)/shard_map/all_gather | solution.py:231
  91.5 8.9 %all-reduce.8 = f32[4]{0:T(128)S(1)} all-reduce(f32[4]{0:T(128)S(1)} %dynamic-update-slice), channel_id=1, replica_groups=mesh['section'=4,'coil'=4,'cuts'=2] {'section'}, use_global_device_ids=true, to_apply=%add.8 | all-reduce | flops 4 | bytes 32
  100.4 7.4 %all_gather.41 = bf16[4,18,128]{2,1,0:T(8,128)(2,1)S(1)} all-gather(bf16[1,18,128]{2,1,0:T(8,128)(2,1)S(1)} %copy-done.38), channel_id=1, replica_groups=mesh['section'=4,'coil'=4,'cuts'=2] {'section'}, dimensions={0}, use_global_device_ids=true | all-gather | bytes 23040 | tf_op jit(solution)/shard_map/all_gather | solution.py:232
  111.6 1.8 copy.168
  113.5 10.2 %convert_bitcast_fusion.3 = bf16[8,40,18,128]{3,2,1,0:T(8,128)(2,1)S(1)} fusion(f32[128]{0:T(128)S(1)} %get-tuple-element.73, bf16[8,40,18,128]{3,1,2,0:T(8,128)(2,1)} %bitcast.650, bf16[4,18,128]{2,1,0:T(8,128)(2,1)S(1)} %all_gather.41, bf16[4,128,18]{1,2,0:T(8,128)(2,1)S(1)} %all_gather.39), kind=kOutput, calls=%fused_computation.111 | convolution fusion | flops 409681920 | bytes 2961920 | tf_op jit(solution)/shard_map/fh,xyhz->xyfz/dot_general | solution.py:134
  125.1 1.7 collective-permute-start.6
  128.5 1.5 collective-permute-start.2
  130.5 5.0 collective-permute-done.2
  135.5 2.8 fusion.196
  138.2 2.0 all_gather.42
  141.1 32.4 %all-gather.8.cloned.1.call-done = bf16[32,80,2,128]{3,1,2,0:T(8,128)(2,1)} async-done(((bf16[8,80,2,128]{3,1,2,0:T(8,128)(2,1)}), bf16[32,80,2,128]{3,1,2,0:T(8,128)(2,1)}) %all-gather.8.cloned.1.call-update) | async-done | bytes 1310736 | tf_op jit(solution)/shard_map/all_gather | solution.py:161
  176.6 1.5 collective-permute-start.7
  178.1 7.3 %collective-permute-done.7 = bf16[16,40,2,128]{3,1,0,2:T(8,128)(2,1)S(1)} collective-permute-done((bf16[16,40,2,128]{3,1,0,2:T(8,128)(2,1)S(1)}, bf16[16,40,2,128]{3,1,0,2:T(8,128)(2,1)S(1)}, u32[]{:S(2)}, u32[]{:S(2)}) %collective-permute-start.7) | collective-permute-done | bytes 327712 | tf_op jit(solution)/shard_map/ppermute | solution.py:28
  186.8 1.5 collective-permute-start.8
  188.3 6.4 %collective-permute-done.8 = bf16[16,40,2,128]{3,1,0,2:T(8,128)(2,1)S(1)} collective-permute-done((bf16[16,40,2,128]{3,1,0,2:T(8,128)(2,1)S(1)}, bf16[16,40,2,128]{3,1,0,2:T(8,128)(2,1)S(1)}, u32[]{:S(2)}, u32[]{:S(2)}) %collective-permute-start.8) | collective-permute-done | bytes 327712 | tf_op jit(solution)/shard_map/ppermute | solution.py:28
  200.3 1.5 collective-permute-start.11
  201.8 1.6 collective-permute-done.11
  207.1 24.2 %reduce-scatter.13.cloned.1.call-done = bf16[8,80,2,128]{3,1,2,0:T(8,128)(2,1)} async-done(((bf16[32,80,2,128]{3,1,2,0:T(8,128)(2,1)}), bf16[8,80,2,128]{3,1,2,0:T(8,128)(2,1)}) %reduce-scatter.13.cloned.1.call-update) | async-done | bytes 327696 | tf_op jit(solution)/shard_map/reduce_scatter | solution.py:144
  231.2 1.8 copy.189
  233.1 10.2 %convert_bitcast_fusion.2 = bf16[8,40,18,128]{3,2,1,0:T(8,128)(2,1)S(1)} fusion(f32[128]{0:T(128)S(1)} %get-tuple-element.75, bf16[8,40,18,128]{3,1,2,0:T(8,128)(2,1)} %bitcast.651, bf16[4,18,128]{2,1,0:T(8,128)(2,1)} %copy-done.32, bf16[4,128,18]{1,2,0:T(8,128)(2,1)} %copy-done.31), kind=kOutput, calls=%fused_computation.110 | convolution fusion | flops 409681920 | bytes 2961920 | tf_op jit(solution)/shard_map/fh,xyhz->xyfz/dot_general | solution.py:134
  243.4 1.4 collective-permute-start.12
  244.8 1.7 collective-permute-start.13
  247.6 1.5 collective-permute-start.9
  249.5 5.0 collective-permute-done.9
  254.5 2.7 fusion.197
  257.3 2.0 all_gather.44
  260.2 31.6 %all-gather.10.cloned.1.call-done = bf16[32,80,2,128]{3,1,2,0:T(8,128)(2,1)} async-done(((bf16[8,80,2,128]{3,1,2,0:T(8,128)(2,1)}), bf16[32,80,2,128]{3,1,2,0:T(8,128)(2,1)}) %all-gather.10.cloned.1.call-update) | async-done | bytes 1310736 | tf_op jit(solution)/shard_map/all_gather | solution.py:161
  294.9 1.5 collective-permute-start.14
  296.4 7.3 %collective-permute-done.14 = bf16[16,40,2,128]{3,1,0,2:T(8,128)(2,1)S(1)} collective-permute-done((bf16[16,40,2,128]{3,1,0,2:T(8,128)(2,1)S(1)}, bf16[16,40,2,128]{3,1,0,2:T(8,128)(2,1)S(1)}, u32[]{:S(2)}, u32[]{:S(2)}) %collective-permute-start.14) | collective-permute-done | bytes 327712 | tf_op jit(solution)/shard_map/ppermute | solution.py:28
  305.1 1.5 collective-permute-start.15
  306.6 6.4 %collective-permute-done.15 = bf16[16,40,2,128]{3,1,0,2:T(8,128)(2,1)S(1)} collective-permute-done((bf16[16,40,2,128]{3,1,0,2:T(8,128)(2,1)S(1)}, bf16[16,40,2,128]{3,1,0,2:T(8,128)(2,1)S(1)}, u32[]{:S(2)}, u32[]{:S(2)}) %collective-permute-start.15) | collective-permute-done | bytes 327712 | tf_op jit(solution)/shard_map/ppermute | solution.py:28
  319.9 1.8 collective-permute-done.18
  325.4 24.1 %reduce-scatter.17.cloned.1.call-done = bf16[8,80,2,128]{3,1,2,0:T(8,128)(2,1)} async-done(((bf16[32,80,2,128]{3,1,2,0:T(8,128)(2,1)}), bf16[8,80,2,128]{3,1,2,0:T(8,128)(2,1)}) %reduce-scatter.17.cloned.1.call-update) | async-done | bytes 327696 | tf_op jit(solution)/shard_map/reduce_scatter | solution.py:144
  349.5 1.8 copy.209
  351.6 10.2 %convert_bitcast_fusion.1 = bf16[8,40,18,128]{3,2,1,0:T(8,128)(2,1)S(1)} fusion(f32[128]{0:T(128)S(1)} %get-tuple-element.74, bf16[8,40,18,128]{3,1,2,0:T(8,128)(2,1)} %bitcast.652, bf16[4,18,128]{2,1,0:T(8,128)(2,1)} %copy-done.32, bf16[4,128,18]{1,2,0:T(8,128)(2,1)} %copy-done.31), kind=kOutput, calls=%fused_computation.109 | convolution fusion | flops 409681920 | bytes 2961920 | tf_op jit(solution)/shard_map/fh,xyhz->xyfz/dot_general | solution.py:134
  361.9 1.4 collective-permute-start.19
  365.6 1.5 collective-permute-start.16
  367.6 5.0 collective-permute-done.16
  372.6 2.7 fusion.198
  375.3 2.0 all_gather.46
  378.2 31.6 %all-gather.12.cloned.1.call-done = bf16[32,80,2,128]{3,1,2,0:T(8,128)(2,1)} async-done(((bf16[8,80,2,128]{3,1,2,0:T(8,128)(2,1)}), bf16[32,80,2,128]{3,1,2,0:T(8,128)(2,1)}) %all-gather.12.cloned.1.call-update) | async-done | bytes 1310736 | tf_op jit(solution)/shard_map/all_gather | solution.py:161
  412.9 1.5 collective-permute-start.21
  414.4 7.3 %collective-permute-done.21 = bf16[16,40,2,128]{3,1,0,2:T(8,128)(2,1)S(1)} collective-permute-done((bf16[16,40,2,128]{3,1,0,2:T(8,128)(2,1)S(1)}, bf16[16,40,2,128]{3,1,0,2:T(8,128)(2,1)S(1)}, u32[]{:S(2)}, u32[]{:S(2)}) %collective-permute-start.21) | collective-permute-done | bytes 327712 | tf_op jit(solution)/shard_map/ppermute | solution.py:28
  423.1 1.5 collective-permute-start.22
  424.6 6.4 %collective-permute-done.22 = bf16[16,40,2,128]{3,1,0,2:T(8,128)(2,1)S(1)} collective-permute-done((bf16[16,40,2,128]{3,1,0,2:T(8,128)(2,1)S(1)}, bf16[16,40,2,128]{3,1,0,2:T(8,128)(2,1)S(1)}, u32[]{:S(2)}, u32[]{:S(2)}) %collective-permute-start.22) | collective-permute-done | bytes 327712 | tf_op jit(solution)/shard_map/ppermute | solution.py:28
  436.6 1.5 collective-permute-start.25
  438.1 1.5 collective-permute-done.25
  443.4 24.2 %reduce-scatter.21.cloned.1.call-done = bf16[8,80,2,128]{3,1,2,0:T(8,128)(2,1)} async-done(((bf16[32,80,2,128]{3,1,2,0:T(8,128)(2,1)}), bf16[8,80,2,128]{3,1,2,0:T(8,128)(2,1)}) %reduce-scatter.21.cloned.1.call-update) | async-done | bytes 327696 | tf_op jit(solution)/shard_map/reduce_scatter | solution.py:144
  467.5 1.8 copy.229
  469.4 10.2 %convert_bitcast_fusion = bf16[8,40,18,128]{3,2,1,0:T(8,128)(2,1)S(1)} fusion(f32[128]{0:T(128)S(1)} %get-tuple-element.76, bf16[8,40,18,128]{3,1,2,0:T(8,128)(2,1)} %bitcast.649, bf16[4,18,128]{2,1,0:T(8,128)(2,1)} %copy-done.32, bf16[4,128,18]{1,2,0:T(8,128)(2,1)} %copy-done.31), kind=kOutput, calls=%fused_computation.108 | convolution fusion | flops 409681920 | bytes 2961920 | tf_op jit(solution)/shard_map/fh,xyhz->xyfz/dot_general | solution.py:134
  479.6 1.3 collective-permute-start.26
  481.0 1.5 collective-permute-start.27
  483.6 1.5 collective-permute-start.23
  485.6 5.0 collective-permute-done.23
  490.6 2.7 fusion.240
  494.6 13.7 %all_to_all.12 = bf16[4,1,8,40,2,128]{5,4,3,2,1,0:T(2,128)(2,1)S(1)} all-to-all(bf16[4,1,8,40,2,128]{5,4,3,2,1,0:T(2,128)(2,1)S(1)} %maximum_bitcast_fusion), channel_id=1, replica_groups=mesh['section'=4,'coil'=4,'cuts'=2] {'section'}, dimensions={0} | all-to-all | bytes 1310720 | tf_op jit(solution)/shard_map/all_to_all | solution.py:255
  (316 shorter events, 77.2 us)
Async XLA Ops:
  6.5 38.8 %all-gather.14.cloned.1.call-start = ((), (), s32[]{:S(2)}) async-start(), calls=%async_computation.20 | async-start | bytes 1638400 | tf_op jit(solution)/shard_map/all_gather | solution.py:161
  10.1 101.5 %reduce-scatter.9.cloned.1.call-start = ((), (), s32[]{:S(2)}) async-start(), calls=%async_computation.9 | async-start | bytes 1638400 | tf_op jit(solution)/shard_map/reduce_scatter | solution.py:144
  12.2 35.2 %copy-start.11 = (bf16[128,128]{1,0:T(8,128)(2,1)}, bf16[128,128]{1,0:T(8,128)(2,1)S(1)}, u32[]{:S(2)}) copy-start(bf16[128,128]{1,0:T(8,128)(2,1)S(1)} %multiply_convert_fusion.2) | copy-start | bytes 98308
  12.5 34.9 %copy-start.15 = (bf16[128,128]{1,0:T(8,128)(2,1)}, bf16[128,128]{1,0:T(8,128)(2,1)S(1)}, u32[]{:S(2)}) copy-start(bf16[128,128]{1,0:T(8,128)(2,1)S(1)} %get-tuple-element.89) | copy-start | bytes 98308
  48.3 8.8 %collective-permute-start = (bf16[16,40,2,128]{3,1,0,2:T(8,128)(2,1)S(1)}, bf16[16,40,2,128]{3,1,0,2:T(8,128)(2,1)S(1)}, u32[]{:S(2)}, u32[]{:S(2)}) collective-permute-start(bf16[16,40,2,128]{3,1,0,2:T(8,128)(2,1)S(1)} %dynamic-slice_bitcast_fusion.8), channel_id=1, source_target_pairs={{0,8},{8,0},{16,24},{24,16},{1,9},{9,1},{17,25},{25,17},{2,10},{10... | collective-permute-start | bytes 983048 | tf_op jit(solution)/shard_map/ppermute | solution.py:28
  50.1 7.2 %copy-start.19 = (bf16[2,32,2,32,1]{1,3,0,4,2:T(8,128)(2,1)}, bf16[2,32,2,32,1]{1,3,0,4,2:T(8,128)(2,1)S(1)}, u32[]{:S(2)}) copy-start(bf16[2,32,2,32,1]{1,3,0,4,2:T(8,128)(2,1)S(1)} %copy.238) | copy-start | bytes 24580
  51.0 6.3 %copy-start.33 = (f32[40,128]{1,0:T(8,128)}, f32[40,128]{1,0:T(8,128)S(1)}, u32[]{:S(2)}) copy-start(f32[40,128]{1,0:T(8,128)S(1)} %convert_bitcast_fusion.4) | copy-start | bytes 61444
  58.4 8.0 %collective-permute-start.1 = (bf16[16,40,2,128]{3,1,0,2:T(8,128)(2,1)S(1)}, bf16[16,40,2,128]{3,1,0,2:T(8,128)(2,1)S(1)}, u32[]{:S(2)}, u32[]{:S(2)}) collective-permute-start(bf16[16,40,2,128]{3,1,0,2:T(8,128)(2,1)S(1)} %dynamic-slice_bitcast_fusion.7), channel_id=1, source_target_pairs={{0,8},{8,0},{16,24},{24,16},{1,9},{9,1},{17,25},{25,17},{2,10},{10... | collective-permute-start | bytes 983048 | tf_op jit(solution)/shard_map/ppermute | solution.py:28
  60.5 7.0 %copy-start.23 = (bf16[128,128]{1,0:T(8,128)(2,1)}, bf16[128,128]{1,0:T(8,128)(2,1)S(1)}, u32[]{:S(2)}) copy-start(bf16[128,128]{1,0:T(8,128)(2,1)S(1)} %get-tuple-element.91) | copy-start | bytes 98308
  60.5 7.0 %copy-start.27 = (bf16[128,128]{1,0:T(8,128)(2,1)}, bf16[128,128]{1,0:T(8,128)(2,1)S(1)}, u32[]{:S(2)}) copy-start(bf16[128,128]{1,0:T(8,128)(2,1)S(1)} %get-tuple-element.92) | copy-start | bytes 98308
  70.6 12.7 %copy-start.37 = (bf16[1,128,18]{1,2,0:T(8,128)(2,1)S(1)}, bf16[1,128,18]{1,2,0:T(8,128)(2,1)}, u32[]{:S(2)}) copy-start(bf16[1,128,18]{1,2,0:T(8,128)(2,1)} %param.13) | copy-start | bytes 13828
  70.6 29.8 %copy-start.38 = (bf16[1,18,128]{2,1,0:T(8,128)(2,1)S(1)}, bf16[1,18,128]{2,1,0:T(8,128)(2,1)}, u32[]{:S(2)}) copy-start(bf16[1,18,128]{2,1,0:T(8,128)(2,1)} %param.15) | copy-start | bytes 13828
  70.7 56.7 %reduce-scatter.11.cloned.1.call-start = ((), (), s32[]{:S(2)}) async-start(), calls=%async_computation.10 | async-start | bytes 491520 | tf_op jit(solution)/shard_map/reduce_scatter | solution.py:150
  70.9 37.0 %collective-permute-start.3 = (bf16[8,1,2,128]{3,2,1,0:T(2,128)(2,1)S(1)}, bf16[8,1,2,128]{3,2,1,0:T(2,128)(2,1)S(1)}, u32[]{:S(2)}, u32[]{:S(2)}) collective-permute-start(bf16[8,1,2,128]{3,2,1,0:T(2,128)(2,1)S(1)} %get-tuple-element.67), channel_id=1, source_target_pairs={{0,1},{2,3},{4,5},{6,7},{8,9},{10,11},{12,13},{14,15},{16,17},{18,... | collective-permute-start | bytes 12296 | tf_op jit(solution)/shard_map/ppermute | solution.py:15
  72.2 35.7 %collective-permute-start.4 = (bf16[8,1,2,128]{3,2,1,0:T(2,128)(2,1)S(1)}, bf16[8,1,2,128]{3,2,1,0:T(2,128)(2,1)S(1)}, u32[]{:S(2)}, u32[]{:S(2)}) collective-permute-start(bf16[8,1,2,128]{3,2,1,0:T(2,128)(2,1)S(1)} %get-tuple-element.68), channel_id=1, source_target_pairs={{1,0},{3,2},{5,4},{7,6},{9,8},{11,10},{13,12},{15,14},{17,16},{19,... | collective-permute-start | bytes 12296 | tf_op jit(solution)/shard_map/ppermute | solution.py:16
  91.5 22.0 %copy-start.31 = (bf16[4,128,18]{1,2,0:T(8,128)(2,1)}, bf16[4,128,18]{1,2,0:T(8,128)(2,1)S(1)}, u32[]{:S(2)}) copy-start(bf16[4,128,18]{1,2,0:T(8,128)(2,1)S(1)} %all_gather.39) | copy-start | bytes 55300
  107.9 5.6 %copy-start.32 = (bf16[4,18,128]{2,1,0:T(8,128)(2,1)}, bf16[4,18,128]{2,1,0:T(8,128)(2,1)S(1)}, u32[]{:S(2)}) copy-start(bf16[4,18,128]{2,1,0:T(8,128)(2,1)S(1)} %all_gather.41) | copy-start | bytes 55300
  113.4 60.1 %all-gather.8.cloned.1.call-start = ((), (), s32[]{:S(2)}) async-start(), calls=%async_computation.11 | async-start | bytes 1638400 | tf_op jit(solution)/shard_map/all_gather | solution.py:161
  123.8 6.2 %collective-permute-start.5 = (bf16[8,1,18,128]{3,2,1,0:T(8,128)(2,1)S(1)}, bf16[8,1,18,128]{3,2,1,0:T(8,128)(2,1)S(1)}, u32[]{:S(2)}, u32[]{:S(2)}) collective-permute-start(bf16[8,1,18,128]{3,2,1,0:T(8,128)(2,1)S(1)} %get-tuple-element.25), channel_id=1, source_target_pairs={{0,1},{2,3},{4,5},{6,7},{8,9},{10,11},{12,13},{14,15},{16,17},{18,... | collective-permute-start | bytes 110600 | tf_op jit(solution)/shard_map/ppermute | solution.py:15
  125.1 4.9 collective-permute-start.6
  128.5 7.0 %copy-start.3 = (bf16[8,40,2,128]{3,0,2,1:T(8,128)(2,1)S(1)}, bf16[8,40,2,128]{3,0,2,1:T(8,128)(2,1)}, u32[]{:S(2)}) copy-start(bf16[8,40,2,128]{3,0,2,1:T(8,128)(2,1)} %reduce-scatter.11.cloned.1.call-done) | copy-start | bytes 491524
  128.5 7.0 %collective-permute-start.2 = (bf16[8,40,2,128]{3,2,1,0:T(2,128)(2,1)S(1)}, bf16[8,40,2,128]{3,2,1,0:T(2,128)(2,1)S(1)}, u32[]{:S(2)}, u32[]{:S(2)}) collective-permute-start(bf16[8,40,2,128]{3,2,1,0:T(2,128)(2,1)S(1)} %copy.169), channel_id=1, source_target_pairs={{0,8},{8,0},{16,24},{24,16},{1,9},{9,1},{17,25},{25,17},{2,10},{10... | collective-permute-start | bytes 491528 | tf_op jit(solution)/shard_map/ppermute | solution.py:28
  141.1 90.2 %reduce-scatter.13.cloned.1.call-start = ((), (), s32[]{:S(2)}) async-start(), calls=%async_computation.12 | async-start | bytes 1638400 | tf_op jit(solution)/shard_map/reduce_scatter | solution.py:144
  176.6 9.0 %copy-start.8 = (bf16[1,1,32,40,2,128]{5,4,3,2,1,0:T(2,128)(2,1)S(1)}, bf16[1,1,32,40,2,128]{5,4,3,2,1,0:T(2,128)(2,1)}, u32[]{:S(2)}) copy-start(bf16[1,1,32,40,2,128]{5,4,3,2,1,0:T(2,128)(2,1)} %copy-done.7) | copy-start | bytes 1966084
  176.6 9.0 %copy-start.20 = (bf16[2,32,2,32,1]{1,3,0,4,2:T(8,128)(2,1)S(1)}, bf16[2,32,2,32,1]{1,3,0,4,2:T(8,128)(2,1)}, u32[]{:S(2)}) copy-start(bf16[2,32,2,32,1]{1,3,0,4,2:T(8,128)(2,1)} %copy-done.19) | copy-start | bytes 24580
  176.6 9.0 %copy-start.34 = (f32[40,128]{1,0:T(8,128)S(1)}, f32[40,128]{1,0:T(8,128)}, u32[]{:S(2)}) copy-start(f32[40,128]{1,0:T(8,128)} %copy-done.33) | copy-start | bytes 61444
  176.6 8.8 %collective-permute-start.7 = (bf16[16,40,2,128]{3,1,0,2:T(8,128)(2,1)S(1)}, bf16[16,40,2,128]{3,1,0,2:T(8,128)(2,1)S(1)}, u32[]{:S(2)}, u32[]{:S(2)}) collective-permute-start(bf16[16,40,2,128]{3,1,0,2:T(8,128)(2,1)S(1)} %dynamic-slice_bitcast_fusion.6), channel_id=1, source_target_pairs={{0,8},{8,0},{16,24},{24,16},{1,9},{9,1},{17,25},{25,17},{2,10},{10... | collective-permute-start | bytes 983048 | tf_op jit(solution)/shard_map/ppermute | solution.py:28
  186.8 7.9 %collective-permute-start.8 = (bf16[16,40,2,128]{3,1,0,2:T(8,128)(2,1)S(1)}, bf16[16,40,2,128]{3,1,0,2:T(8,128)(2,1)S(1)}, u32[]{:S(2)}, u32[]{:S(2)}) collective-permute-start(bf16[16,40,2,128]{3,1,0,2:T(8,128)(2,1)S(1)} %dynamic-slice_bitcast_fusion.5), channel_id=1, source_target_pairs={{0,8},{8,0},{16,24},{24,16},{1,9},{9,1},{17,25},{25,17},{2,10},{10... | collective-permute-start | bytes 983048 | tf_op jit(solution)/shard_map/ppermute | solution.py:28
  199.0 47.5 %reduce-scatter.15.cloned.1.call-start = ((), (), s32[]{:S(2)}) async-start(), calls=%async_computation.13 | async-start | bytes 491520 | tf_op jit(solution)/shard_map/reduce_scatter | solution.py:150
  199.0 2.8 collective-permute-start.10
  200.3 3.1 collective-permute-start.11
  233.1 58.7 %all-gather.10.cloned.1.call-start = ((), (), s32[]{:S(2)}) async-start(), calls=%async_computation.14 | async-start | bytes 1638400 | tf_op jit(solution)/shard_map/all_gather | solution.py:161
  243.4 5.7 %collective-permute-start.12 = (bf16[8,1,18,128]{3,2,1,0:T(8,128)(2,1)S(1)}, bf16[8,1,18,128]{3,2,1,0:T(8,128)(2,1)S(1)}, u32[]{:S(2)}, u32[]{:S(2)}) collective-permute-start(bf16[8,1,18,128]{3,2,1,0:T(8,128)(2,1)S(1)} %get-tuple-element.21), channel_id=1, source_target_pairs={{0,1},{2,3},{4,5},{6,7},{8,9},{10,11},{12,13},{14,15},{16,17},{18,... | collective-permute-start | bytes 110600 | tf_op jit(solution)/shard_map/ppermute | solution.py:15
  244.8 4.3 collective-permute-start.13
  247.6 7.0 %copy-start.5 = (bf16[8,40,2,128]{3,0,2,1:T(8,128)(2,1)S(1)}, bf16[8,40,2,128]{3,0,2,1:T(8,128)(2,1)}, u32[]{:S(2)}) copy-start(bf16[8,40,2,128]{3,0,2,1:T(8,128)(2,1)} %reduce-scatter.15.cloned.1.call-done) | copy-start | bytes 491524
  247.6 7.0 %collective-permute-start.9 = (bf16[8,40,2,128]{3,2,1,0:T(2,128)(2,1)S(1)}, bf16[8,40,2,128]{3,2,1,0:T(2,128)(2,1)S(1)}, u32[]{:S(2)}, u32[]{:S(2)}) collective-permute-start(bf16[8,40,2,128]{3,2,1,0:T(2,128)(2,1)S(1)} %copy.190), channel_id=1, source_target_pairs={{0,8},{8,0},{16,24},{24,16},{1,9},{9,1},{17,25},{25,17},{2,10},{10... | collective-permute-start | bytes 491528 | tf_op jit(solution)/shard_map/ppermute | solution.py:28
  260.1 89.4 %reduce-scatter.17.cloned.1.call-start = ((), (), s32[]{:S(2)}) async-start(), calls=%async_computation.15 | async-start | bytes 1638400 | tf_op jit(solution)/shard_map/reduce_scatter | solution.py:144
  294.8 9.1 %copy-start.9 = (bf16[1,1,32,40,2,128]{5,4,3,2,1,0:T(2,128)(2,1)S(1)}, bf16[1,1,32,40,2,128]{5,4,3,2,1,0:T(2,128)(2,1)}, u32[]{:S(2)}) copy-start(bf16[1,1,32,40,2,128]{5,4,3,2,1,0:T(2,128)(2,1)} %copy-done.7) | copy-start | bytes 1966084
  294.8 9.1 %copy-start.21 = (bf16[2,32,2,32,1]{1,3,0,4,2:T(8,128)(2,1)S(1)}, bf16[2,32,2,32,1]{1,3,0,4,2:T(8,128)(2,1)}, u32[]{:S(2)}) copy-start(bf16[2,32,2,32,1]{1,3,0,4,2:T(8,128)(2,1)} %copy-done.19) | copy-start | bytes 24580
  294.9 9.1 %copy-start.35 = (f32[40,128]{1,0:T(8,128)S(1)}, f32[40,128]{1,0:T(8,128)}, u32[]{:S(2)}) copy-start(f32[40,128]{1,0:T(8,128)} %copy-done.33) | copy-start | bytes 61444
  294.9 8.8 %collective-permute-start.14 = (bf16[16,40,2,128]{3,1,0,2:T(8,128)(2,1)S(1)}, bf16[16,40,2,128]{3,1,0,2:T(8,128)(2,1)S(1)}, u32[]{:S(2)}, u32[]{:S(2)}) collective-permute-start(bf16[16,40,2,128]{3,1,0,2:T(8,128)(2,1)S(1)} %dynamic-slice_bitcast_fusion.4), channel_id=1, source_target_pairs={{0,8},{8,0},{16,24},{24,16},{1,9},{9,1},{17,25},{25,17},{2,10},{10... | collective-permute-start | bytes 983048 | tf_op jit(solution)/shard_map/ppermute | solution.py:28
  305.1 8.0 %collective-permute-start.15 = (bf16[16,40,2,128]{3,1,0,2:T(8,128)(2,1)S(1)}, bf16[16,40,2,128]{3,1,0,2:T(8,128)(2,1)S(1)}, u32[]{:S(2)}, u32[]{:S(2)}) collective-permute-start(bf16[16,40,2,128]{3,1,0,2:T(8,128)(2,1)S(1)} %dynamic-slice_bitcast_fusion.3), channel_id=1, source_target_pairs={{0,8},{8,0},{16,24},{24,16},{1,9},{9,1},{17,25},{25,17},{2,10},{10... | collective-permute-start | bytes 983048 | tf_op jit(solution)/shard_map/ppermute | solution.py:28
  317.3 47.3 %reduce-scatter.19.cloned.1.call-start = ((), (), s32[]{:S(2)}) async-start(), calls=%async_computation.16 | async-start | bytes 491520 | tf_op jit(solution)/shard_map/reduce_scatter | solution.py:150
  317.3 2.6 collective-permute-start.17
  318.6 3.1 collective-permute-start.18
  351.4 58.5 %all-gather.12.cloned.1.call-start = ((), (), s32[]{:S(2)}) async-start(), calls=%async_computation.17 | async-start | bytes 1638400 | tf_op jit(solution)/shard_map/all_gather | solution.py:161
  361.9 5.3 %collective-permute-start.19 = (bf16[8,1,18,128]{3,2,1,0:T(8,128)(2,1)S(1)}, bf16[8,1,18,128]{3,2,1,0:T(8,128)(2,1)S(1)}, u32[]{:S(2)}, u32[]{:S(2)}) collective-permute-start(bf16[8,1,18,128]{3,2,1,0:T(8,128)(2,1)S(1)} %get-tuple-element.15), channel_id=1, source_target_pairs={{0,1},{2,3},{4,5},{6,7},{8,9},{10,11},{12,13},{14,15},{16,17},{18,... | collective-permute-start | bytes 110600 | tf_op jit(solution)/shard_map/ppermute | solution.py:15
  363.2 3.9 collective-permute-start.20
  365.6 7.0 %copy-start.6 = (bf16[8,40,2,128]{3,0,2,1:T(8,128)(2,1)S(1)}, bf16[8,40,2,128]{3,0,2,1:T(8,128)(2,1)}, u32[]{:S(2)}) copy-start(bf16[8,40,2,128]{3,0,2,1:T(8,128)(2,1)} %reduce-scatter.19.cloned.1.call-done) | copy-start | bytes 491524
  365.6 7.0 %collective-permute-start.16 = (bf16[8,40,2,128]{3,2,1,0:T(2,128)(2,1)S(1)}, bf16[8,40,2,128]{3,2,1,0:T(2,128)(2,1)S(1)}, u32[]{:S(2)}, u32[]{:S(2)}) collective-permute-start(bf16[8,40,2,128]{3,2,1,0:T(2,128)(2,1)S(1)} %copy.210), channel_id=1, source_target_pairs={{0,8},{8,0},{16,24},{24,16},{1,9},{9,1},{17,25},{25,17},{2,10},{10... | collective-permute-start | bytes 491528 | tf_op jit(solution)/shard_map/ppermute | solution.py:28
  378.1 89.4 %reduce-scatter.21.cloned.1.call-start = ((), (), s32[]{:S(2)}) async-start(), calls=%async_computation.18 | async-start | bytes 1638400 | tf_op jit(solution)/shard_map/reduce_scatter | solution.py:144
  412.9 9.0 %copy-start.10 = (bf16[1,1,32,40,2,128]{5,4,3,2,1,0:T(2,128)(2,1)S(1)}, bf16[1,1,32,40,2,128]{5,4,3,2,1,0:T(2,128)(2,1)}, u32[]{:S(2)}) copy-start(bf16[1,1,32,40,2,128]{5,4,3,2,1,0:T(2,128)(2,1)} %copy-done.7) | copy-start | bytes 1966084
  412.9 9.0 %copy-start.22 = (bf16[2,32,2,32,1]{1,3,0,4,2:T(8,128)(2,1)S(1)}, bf16[2,32,2,32,1]{1,3,0,4,2:T(8,128)(2,1)}, u32[]{:S(2)}) copy-start(bf16[2,32,2,32,1]{1,3,0,4,2:T(8,128)(2,1)} %copy-done.19) | copy-start | bytes 24580
  412.9 9.0 %copy-start.36 = (f32[40,128]{1,0:T(8,128)S(1)}, f32[40,128]{1,0:T(8,128)}, u32[]{:S(2)}) copy-start(f32[40,128]{1,0:T(8,128)} %copy-done.33) | copy-start | bytes 61444
  412.9 8.8 %collective-permute-start.21 = (bf16[16,40,2,128]{3,1,0,2:T(8,128)(2,1)S(1)}, bf16[16,40,2,128]{3,1,0,2:T(8,128)(2,1)S(1)}, u32[]{:S(2)}, u32[]{:S(2)}) collective-permute-start(bf16[16,40,2,128]{3,1,0,2:T(8,128)(2,1)S(1)} %dynamic-slice_bitcast_fusion.2), channel_id=1, source_target_pairs={{0,8},{8,0},{16,24},{24,16},{1,9},{9,1},{17,25},{25,17},{2,10},{10... | collective-permute-start | bytes 983048 | tf_op jit(solution)/shard_map/ppermute | solution.py:28
  423.1 7.9 %collective-permute-start.22 = (bf16[16,40,2,128]{3,1,0,2:T(8,128)(2,1)S(1)}, bf16[16,40,2,128]{3,1,0,2:T(8,128)(2,1)S(1)}, u32[]{:S(2)}, u32[]{:S(2)}) collective-permute-start(bf16[16,40,2,128]{3,1,0,2:T(8,128)(2,1)S(1)} %dynamic-slice_bitcast_fusion.1), channel_id=1, source_target_pairs={{0,8},{8,0},{16,24},{24,16},{1,9},{9,1},{17,25},{25,17},{2,10},{10... | collective-permute-start | bytes 983048 | tf_op jit(solution)/shard_map/ppermute | solution.py:28
  435.3 47.3 %reduce-scatter.23.cloned.1.call-start = ((), (), s32[]{:S(2)}) async-start(), calls=%async_computation.19 | async-start | bytes 491520 | tf_op jit(solution)/shard_map/reduce_scatter | solution.py:150
  435.3 2.8 collective-permute-start.24
  436.6 3.1 collective-permute-start.25
  479.6 5.5 %collective-permute-start.26 = (bf16[8,1,18,128]{3,2,1,0:T(8,128)(2,1)S(1)}, bf16[8,1,18,128]{3,2,1,0:T(8,128)(2,1)S(1)}, u32[]{:S(2)}, u32[]{:S(2)}) collective-permute-start(bf16[8,1,18,128]{3,2,1,0:T(8,128)(2,1)S(1)} %get-tuple-element.9), channel_id=1, source_target_pairs={{0,1},{2,3},{4,5},{6,7},{8,9},{10,11},{12,13},{14,15},{16,17},{18,... | collective-permute-start | bytes 110600 | tf_op jit(solution)/shard_map/ppermute | solution.py:15
  481.0 4.2 collective-permute-start.27
  483.6 7.0 %copy-start.4 = (bf16[8,40,2,128]{3,0,2,1:T(8,128)(2,1)S(1)}, bf16[8,40,2,128]{3,0,2,1:T(8,128)(2,1)}, u32[]{:S(2)}) copy-start(bf16[8,40,2,128]{3,0,2,1:T(8,128)(2,1)} %reduce-scatter.23.cloned.1.call-done) | copy-start | bytes 491524
  483.6 7.0 %collective-permute-start.23 = (bf16[8,40,2,128]{3,2,1,0:T(2,128)(2,1)S(1)}, bf16[8,40,2,128]{3,2,1,0:T(2,128)(2,1)S(1)}, u32[]{:S(2)}, u32[]{:S(2)}) collective-permute-start(bf16[8,40,2,128]{3,2,1,0:T(2,128)(2,1)S(1)} %copy.230), channel_id=1, source_target_pairs={{0,8},{8,0},{16,24},{24,16},{1,9},{9,1},{17,25},{25,17},{2,10},{10... | collective-permute-start | bytes 491528 | tf_op jit(solution)/shard_map/ppermute | solution.py:28
  493.3 15.8 %copy-start.1 = (bf16[2,1,32,80,2,128]{5,4,3,2,1,0:T(2,128)(2,1)S(1)}, bf16[2,1,32,80,2,128]{5,4,3,2,1,0:T(2,128)(2,1)}, u32[]{:S(2)}) copy-start(bf16[2,1,32,80,2,128]{5,4,3,2,1,0:T(2,128)(2,1)} %param.9) | copy-start | bytes 7864324
  (17 other events, 30.4 us)
Sparse Core Ops, SparseCore 0:
  10.2 35.1 all-gather.13
  70.8 32.0 reduce-scatter.8
  113.6 7.5 reduce-scatter.10
  141.2 32.3 all-gather.7
  199.1 32.1 reduce-scatter.12
  233.3 6.4 reduce-scatter.14
  260.2 31.5 all-gather.9
  317.4 32.0 reduce-scatter.16
  351.8 6.4 reduce-scatter.18
  378.3 31.5 all-gather.11
  435.4 32.1 reduce-scatter.20
  469.6 6.4 reduce-scatter.22
where the time goes:
time: 525 us; the launch traced here: 516 us
  waiting for transfers between devices  278 us (53%)
  blocking collectives  54.4 us (10%)
  matrix products  49.7 us (9%)
  local copies, waits for them, and re-layouts  44.4 us (8%)
  starting transfers between devices  41.4 us (8%)
  other arithmetic  32.6 us (6%)
  between operations  16.4 us (3%)
    all_gather x4, waiting for transfers between devices, pair_block(): whole = lax.all_gather(halves, 'coil', axis=0, tiled=True)  129 us
    reduce_scatter x4, waiting for transfers between devices, sum_gradient(): lax.psum_scatter(back_rows(jnp.int32(0), lax.axis_size('coil') * current....  72.5 us
    ppermute x12, waiting for transfers between devices, from_partner(): return lax.ppermute(block, axis, route)  71.4 us
    dot_general x4, matrix products, refine_rows(): jnp.einsum('fh,xyhz->xyfz', weights_out, hidden, preferred_element_type=j...  40.9 us
    ppermute x12, starting transfers between devices, from_partner(): return lax.ppermute(block, axis, route)  18.4 us
    all_to_all x1, blocking collectives, body(): lax.all_to_all(stacked, 'section', split_axis=0, concat_axis=1, tiled=True)  13.7 us
    ppermute x8, starting transfers between devices, extended_2(): after = lax.ppermute(leading, axis, down)  11.8 us
    ppermute x8, starting transfers between devices, extended_2(): before = lax.ppermute(last, axis, up)  10.5 us
  transfers between devices with their start and end apart: 40, of which 22 were waited for; matrix products, arithmetic and copies ran while one was open for 13% of the time, Pallas kernels for 0%

commit v1 on v0

--- a/solution.py
+++ b/solution.py
@@ -158,7 +158,19 @@
 
 def pair_block(current, sens_one, data_one, mask_one, step, weights_in, bias, weights_out, half):
     halves = whole_rows(current)
-    whole = lax.all_gather(halves, "coil", axis=0, tiled=True)
+    devs = lax.axis_size("coil")
+    pile = [(d, (d + 1) % devs) for d in range(devs)]
+    views = [(d, (d - 1) % devs) for d in range(devs)]
+    top, all_values = ([halves], [halves])
+    for _ in range(devs // 2):
+        top.append(lax.ppermute(top[-1], "coil", pile))
+    for _ in range((devs - 1) // 2):
+        all_values.append(lax.ppermute(all_values[-1], "coil", views))
+    whole = jnp.roll(
+        jnp.concatenate([*top[::-1], *all_values[1:]], 0),
+        (lax.axis_index("coil") - devs // 2) * halves.shape[0],
+        0,
+    )
     size_x, size_y, _, size_z = whole.shape
     half_x = size_x // 2
     half_y = size_y // 2

time: 525 us -> 496 us (0.945)
  waiting for transfers between devices: 278 us -> 230 us
  starting transfers between devices: 41.4 us -> 59.2 us
  other arithmetic: 32.6 us -> 26.6 us
    all_gather x4 -> x0, waiting for transfers between devices: 129 us -> none  [pair_block(): whole = lax.all_gather(halves, 'coil', axis=0, tiled=True)]
    ppermute x0 -> x12, waiting for transfers between devices: none -> 87 us  [the longest x8 74.6 us: pair_block(): top.append(lax.ppermute(top[-1], 'coil', pile))]
    ppermute x0 -> x12, starting transfers between devices: none -> 18.7 us  [the longest x4 16.4 us: pair_block(): all_values.append(lax.ppermute(all_values[-1], 'coil', views))]
    dot_general x0 -> x4, local copies, waits for them, and re-layouts: none -> 6.95 us  [refine_rows(): jnp.einsum('fh,xyhz->xyfz', weights_out, hidden, preferred_element_type=j...]
  transfers between devices with their start and end apart: 40 -> 48, of which waited for: 22 -> 29; matrix products, arithmetic and copies ran while one was open for 13% -> 16% of each run, Pallas kernels for 0% -> 0%
where the time goes in v1:
time: 496 us; the launch traced here: 487 us
  waiting for transfers between devices  230 us (46%)
  starting transfers between devices  59.2 us (12%)
  blocking collectives  54.5 us (11%)
  matrix products  54 us (11%)
  local copies, waits for them, and re-layouts  46.6 us (9%)
  other arithmetic  26.6 us (5%)
  between operations  16.3 us (3%)
    ppermute x8, waiting for transfers between devices, pair_block(): top.append(lax.ppermute(top[-1], 'coil', pile))  74.6 us
    ppermute x12, waiting for transfers between devices, from_partner(): return lax.ppermute(block, axis, route)  69.4 us
    reduce_scatter x4, waiting for transfers between devices, sum_gradient(): lax.psum_scatter(back_rows(jnp.int32(0), lax.axis_size('coil') * current....  68 us
    dot_general x4, matrix products, refine_rows(): jnp.einsum('fh,xyhz->xyfz', weights_out, hidden, preferred_element_type=j...  45.2 us
    ppermute x12, starting transfers between devices, from_partner(): return lax.ppermute(block, axis, route)  18.4 us
    ppermute x4, starting transfers between devices, pair_block(): all_values.append(lax.ppermute(all_values[-1], 'coil', views))  16.4 us
    all_to_all x1, blocking collectives, body(): lax.all_to_all(stacked, 'section', split_axis=0, concat_axis=1, tiled=True)  13.8 us
    ppermute x4, waiting for transfers between devices, pair_block(): all_values.append(lax.ppermute(all_values[-1], 'coil', views))  12.4 us
  transfers between devices with their start and end apart: 48, of which 29 were waited for; matrix products, arithmetic and copies ran while one was open for 16% of the time, Pallas kernels for 0%

profile of v1, /device:TPU:0, one launch (start us, length us, event | category | flops | bytes accessed | tf_op | source)
XLA Modules:
  0.0 486.8 jit_solution(6343493376962927894)
XLA Ops:
  7.8 2.2 all-gather
  9.9 5.0 %collective-permute-start.2 = (bf16[8,80,2,128]{3,1,2,0:T(8,128)(2,1)S(1)}, bf16[8,80,2,128]{3,1,2,0:T(8,128)(2,1)}, u32[]{:S(2)}, u32[]{:S(2)}) collective-permute-start(bf16[8,80,2,128]{3,1,2,0:T(8,128)(2,1)S(1)} %bitcast.658), channel_id=1, source_target_pairs={{0,6},{2,0},{4,2},{6,4},{1,7},{3,1},{5,3},{7,5},{8,14},{10,8},{12,... | collective-permute-start | bytes 983048 | tf_op jit(solution)/shard_map/ppermute | solution.py:168
  16.6 13.6 %collective-permute-done = bf16[8,80,2,128]{3,1,2,0:T(8,128)(2,1)} collective-permute-done((bf16[8,80,2,128]{3,1,2,0:T(8,128)(2,1)S(1)}, bf16[8,80,2,128]{3,1,2,0:T(8,128)(2,1)}, u32[]{:S(2)}, u32[]{:S(2)}) %collective-permute-start) | collective-permute-done | bytes 327712 | tf_op jit(solution)/shard_map/ppermute | solution.py:166
  30.2 1.6 collective-permute-start.1
  32.5 8.6 %collective-permute-done.1 = bf16[8,80,2,128]{3,1,2,0:T(8,128)(2,1)S(1)} collective-permute-done((bf16[8,80,2,128]{3,1,2,0:T(8,128)(2,1)}, bf16[8,80,2,128]{3,1,2,0:T(8,128)(2,1)S(1)}, u32[]{:S(2)}, u32[]{:S(2)}) %collective-permute-start.1) | collective-permute-done | bytes 327712 | tf_op jit(solution)/shard_map/ppermute | solution.py:166
  41.1 2.0 fusion.101
  44.8 1.6 collective-permute-start.3
  47.6 1.6 constant_dynamic-slice_fusion
  49.2 3.8 collective-permute-done.3
  54.3 1.6 collective-permute-start.4
  56.4 5.2 %collective-permute-done.4 = bf16[16,40,2,128]{3,1,0,2:T(8,128)(2,1)S(1)} collective-permute-done((bf16[16,40,2,128]{3,1,0,2:T(8,128)(2,1)S(1)}, bf16[16,40,2,128]{3,1,0,2:T(8,128)(2,1)S(1)}, u32[]{:S(2)}, u32[]{:S(2)}) %collective-permute-start.4) | collective-permute-done | bytes 327712 | tf_op jit(solution)/shard_map/ppermute | solution.py:28
  70.5 7.9 %all-gather.1 = f32[4,1,128]{2,1,0:T(1,128)S(1)} all-gather(f32[1,1,128]{2,1,0:T(1,128)S(1)} %bitcast.673), channel_id=1, replica_groups=mesh['section'=4,'coil'=4,'cuts'=2] {'section'}, dimensions={0}, use_global_device_ids=true | all-gather | bytes 2560 | tf_op jit(solution)/shard_map/all_gather | solution.py:240
  79.0 8.1 %all_gather.26 = bf16[4,128,18]{1,2,0:T(8,128)(2,1)S(1)} all-gather(bf16[1,128,18]{1,2,0:T(8,128)(2,1)S(1)} %copy-done.24), channel_id=1, replica_groups=mesh['section'=4,'coil'=4,'cuts'=2] {'section'}, dimensions={0}, use_global_device_ids=true | all-gather | bytes 23040 | tf_op jit(solution)/shard_map/all_gather | solution.py:243
  87.2 8.9 %all-reduce.8 = f32[4]{0:T(128)S(1)} all-reduce(f32[4]{0:T(128)S(1)} %dynamic-update-slice), channel_id=1, replica_groups=mesh['section'=4,'coil'=4,'cuts'=2] {'section'}, use_global_device_ids=true, to_apply=%add.8 | all-reduce | flops 4 | bytes 32
  96.1 7.4 %all_gather.28 = bf16[4,18,128]{2,1,0:T(8,128)(2,1)S(1)} all-gather(bf16[1,18,128]{2,1,0:T(8,128)(2,1)S(1)} %copy-done.25), channel_id=1, replica_groups=mesh['section'=4,'coil'=4,'cuts'=2] {'section'}, dimensions={0}, use_global_device_ids=true | all-gather | bytes 23040 | tf_op jit(solution)/shard_map/all_gather | solution.py:244
  106.2 1.8 copy.298
  108.1 11.3 %fusion.22 = bf16[8,40,128,18]{2,3,1,0:T(8,128)(2,1)} fusion(f32[128]{0:T(128)S(1)} %get-tuple-element.76, bf16[8,40,18,128]{3,1,2,0:T(8,128)(2,1)} %bitcast.655, bf16[4,18,128]{2,1,0:T(8,128)(2,1)S(1)} %all_gather.28, bf16[4,128,18]{1,2,0:T(8,128)(2,1)S(1)} %all_gather.26), kind=kOutput, calls=%fused_computation.51 | convolution fusion | flops 408944640 | bytes 2961920 | tf_op jit(solution)/shard_map/fh,xyhz->xyfz/dot_general | solution.py:134
  119.4 1.7 copy.622
  125.5 1.5 collective-permute-start.5
  127.8 4.6 collective-permute-done.5
  133.7 2.0 all_gather.29
  135.8 3.8 collective-permute-start.12
  139.6 8.6 %collective-permute-done.10 = bf16[8,80,2,128]{3,1,2,0:T(8,128)(2,1)S(1)} collective-permute-done((bf16[8,80,2,128]{3,1,2,0:T(8,128)(2,1)S(1)}, bf16[8,80,2,128]{3,1,2,0:T(8,128)(2,1)S(1)}, u32[]{:S(2)}, u32[]{:S(2)}) %collective-permute-start.10) | collective-permute-done | bytes 327712 | tf_op jit(solution)/shard_map/ppermute | solution.py:166
  148.4 4.1 collective-permute-done.12
  152.6 8.9 %collective-permute-done.11 = bf16[8,80,2,128]{3,1,2,0:T(8,128)(2,1)S(1)} collective-permute-done((bf16[8,80,2,128]{3,1,2,0:T(8,128)(2,1)S(1)}, bf16[8,80,2,128]{3,1,2,0:T(8,128)(2,1)S(1)}, u32[]{:S(2)}, u32[]{:S(2)}) %collective-permute-start.11) | collective-permute-done | bytes 327712 | tf_op jit(solution)/shard_map/ppermute | solution.py:166
  164.4 1.5 collective-permute-start.13
  165.9 7.4 %collective-permute-done.13 = bf16[16,40,2,128]{3,1,0,2:T(8,128)(2,1)S(1)} collective-permute-done((bf16[16,40,2,128]{3,1,0,2:T(8,128)(2,1)S(1)}, bf16[16,40,2,128]{3,1,0,2:T(8,128)(2,1)S(1)}, u32[]{:S(2)}, u32[]{:S(2)}) %collective-permute-start.13) | collective-permute-done | bytes 327712 | tf_op jit(solution)/shard_map/ppermute | solution.py:28
  176.2 6.6 %collective-permute-done.14 = bf16[16,40,2,128]{3,1,0,2:T(8,128)(2,1)S(1)} collective-permute-done((bf16[16,40,2,128]{3,1,0,2:T(8,128)(2,1)S(1)}, bf16[16,40,2,128]{3,1,0,2:T(8,128)(2,1)S(1)}, u32[]{:S(2)}, u32[]{:S(2)}) %collective-permute-start.14) | collective-permute-done | bytes 327712 | tf_op jit(solution)/shard_map/ppermute | solution.py:28
  189.7 1.8 collective-permute-done.17
  194.1 22.8 %reduce-scatter.13.cloned.1.call-done = bf16[8,80,2,128]{3,1,2,0:T(8,128)(2,1)} async-done(((bf16[32,80,2,128]{3,1,2,0:T(8,128)(2,1)}), bf16[8,80,2,128]{3,1,2,0:T(8,128)(2,1)}) %reduce-scatter.13.cloned.1.call-update) | async-done | bytes 327696 | tf_op jit(solution)/shard_map/reduce_scatter | solution.py:144
  216.9 1.8 copy.318
  219.3 11.3 %fusion.20 = bf16[8,40,128,18]{2,3,1,0:T(8,128)(2,1)} fusion(f32[128]{0:T(128)S(1)} %copy-done.28, bf16[8,40,18,128]{3,1,2,0:T(8,128)(2,1)} %bitcast.656, bf16[4,18,128]{2,1,0:T(8,128)(2,1)S(1)} %all_gather.28, bf16[4,128,18]{1,2,0:T(8,128)(2,1)S(1)} %all_gather.26), kind=kOutput, calls=%fused_computation.50 | convolution fusion | flops 408944640 | bytes 2961920 | tf_op jit(solution)/shard_map/fh,xyhz->xyfz/dot_general | solution.py:134
  230.6 1.7 copy.623
  236.1 1.6 collective-permute-start.15
  238.5 4.6 collective-permute-done.15
  244.3 2.0 all_gather.30
  246.3 3.8 collective-permute-start.22
  250.2 8.6 %collective-permute-done.20 = bf16[8,80,2,128]{3,1,2,0:T(8,128)(2,1)S(1)} collective-permute-done((bf16[8,80,2,128]{3,1,2,0:T(8,128)(2,1)S(1)}, bf16[8,80,2,128]{3,1,2,0:T(8,128)(2,1)S(1)}, u32[]{:S(2)}, u32[]{:S(2)}) %collective-permute-start.20) | collective-permute-done | bytes 327712 | tf_op jit(solution)/shard_map/ppermute | solution.py:166
  258.9 4.2 collective-permute-done.22
  263.1 8.9 %collective-permute-done.21 = bf16[8,80,2,128]{3,1,2,0:T(8,128)(2,1)S(1)} collective-permute-done((bf16[8,80,2,128]{3,1,2,0:T(8,128)(2,1)S(1)}, bf16[8,80,2,128]{3,1,2,0:T(8,128)(2,1)S(1)}, u32[]{:S(2)}, u32[]{:S(2)}) %collective-permute-start.21) | collective-permute-done | bytes 327712 | tf_op jit(solution)/shard_map/ppermute | solution.py:166
  274.8 1.6 collective-permute-start.23
  276.3 7.4 %collective-permute-done.23 = bf16[16,40,2,128]{3,1,0,2:T(8,128)(2,1)S(1)} collective-permute-done((bf16[16,40,2,128]{3,1,0,2:T(8,128)(2,1)S(1)}, bf16[16,40,2,128]{3,1,0,2:T(8,128)(2,1)S(1)}, u32[]{:S(2)}, u32[]{:S(2)}) %collective-permute-start.23) | collective-permute-done | bytes 327712 | tf_op jit(solution)/shard_map/ppermute | solution.py:28
  285.1 1.5 collective-permute-start.24
  286.6 6.6 %collective-permute-done.24 = bf16[16,40,2,128]{3,1,0,2:T(8,128)(2,1)S(1)} collective-permute-done((bf16[16,40,2,128]{3,1,0,2:T(8,128)(2,1)S(1)}, bf16[16,40,2,128]{3,1,0,2:T(8,128)(2,1)S(1)}, u32[]{:S(2)}, u32[]{:S(2)}) %collective-permute-start.24) | collective-permute-done | bytes 327712 | tf_op jit(solution)/shard_map/ppermute | solution.py:28
  300.1 1.8 collective-permute-done.27
  304.5 22.6 %reduce-scatter.17.cloned.1.call-done = bf16[8,80,2,128]{3,1,2,0:T(8,128)(2,1)} async-done(((bf16[32,80,2,128]{3,1,2,0:T(8,128)(2,1)}), bf16[8,80,2,128]{3,1,2,0:T(8,128)(2,1)}) %reduce-scatter.17.cloned.1.call-update) | async-done | bytes 327696 | tf_op jit(solution)/shard_map/reduce_scatter | solution.py:144
  327.1 1.8 copy.338
  329.2 11.3 %fusion.18 = bf16[8,40,128,18]{2,3,1,0:T(8,128)(2,1)} fusion(f32[128]{0:T(128)S(1)} %copy-done.27, bf16[8,40,18,128]{3,1,2,0:T(8,128)(2,1)} %bitcast.657, bf16[4,18,128]{2,1,0:T(8,128)(2,1)S(1)} %all_gather.28, bf16[4,128,18]{1,2,0:T(8,128)(2,1)S(1)} %all_gather.26), kind=kOutput, calls=%fused_computation.49 | convolution fusion | flops 408944640 | bytes 2961920 | tf_op jit(solution)/shard_map/fh,xyhz->xyfz/dot_general | solution.py:134
  340.5 1.7 copy.624
  348.4 4.6 collective-permute-done.25
  354.2 2.0 all_gather.31
  356.3 3.8 collective-permute-start.32
  360.1 8.6 %collective-permute-done.30 = bf16[8,80,2,128]{3,1,2,0:T(8,128)(2,1)S(1)} collective-permute-done((bf16[8,80,2,128]{3,1,2,0:T(8,128)(2,1)S(1)}, bf16[8,80,2,128]{3,1,2,0:T(8,128)(2,1)S(1)}, u32[]{:S(2)}, u32[]{:S(2)}) %collective-permute-start.30) | collective-permute-done | bytes 327712 | tf_op jit(solution)/shard_map/ppermute | solution.py:166
  368.9 4.1 collective-permute-done.32
  373.0 8.9 %collective-permute-done.31 = bf16[8,80,2,128]{3,1,2,0:T(8,128)(2,1)S(1)} collective-permute-done((bf16[8,80,2,128]{3,1,2,0:T(8,128)(2,1)S(1)}, bf16[8,80,2,128]{3,1,2,0:T(8,128)(2,1)S(1)}, u32[]{:S(2)}, u32[]{:S(2)}) %collective-permute-start.31) | collective-permute-done | bytes 327712 | tf_op jit(solution)/shard_map/ppermute | solution.py:166
  386.4 7.5 %collective-permute-done.33 = bf16[16,40,2,128]{3,1,0,2:T(8,128)(2,1)S(1)} collective-permute-done((bf16[16,40,2,128]{3,1,0,2:T(8,128)(2,1)S(1)}, bf16[16,40,2,128]{3,1,0,2:T(8,128)(2,1)S(1)}, u32[]{:S(2)}, u32[]{:S(2)}) %collective-permute-start.33) | collective-permute-done | bytes 327712 | tf_op jit(solution)/shard_map/ppermute | solution.py:28
  396.7 6.6 %collective-permute-done.34 = bf16[16,40,2,128]{3,1,0,2:T(8,128)(2,1)S(1)} collective-permute-done((bf16[16,40,2,128]{3,1,0,2:T(8,128)(2,1)S(1)}, bf16[16,40,2,128]{3,1,0,2:T(8,128)(2,1)S(1)}, u32[]{:S(2)}, u32[]{:S(2)}) %collective-permute-start.34) | collective-permute-done | bytes 327712 | tf_op jit(solution)/shard_map/ppermute | solution.py:28
  409.0 1.6 collective-permute-start.37
  414.6 22.6 %reduce-scatter.21.cloned.1.call-done = bf16[8,80,2,128]{3,1,2,0:T(8,128)(2,1)} async-done(((bf16[32,80,2,128]{3,1,2,0:T(8,128)(2,1)}), bf16[8,80,2,128]{3,1,2,0:T(8,128)(2,1)}) %reduce-scatter.21.cloned.1.call-update) | async-done | bytes 327696 | tf_op jit(solution)/shard_map/reduce_scatter | solution.py:144
  437.2 1.8 copy.358
  439.1 11.3 %fusion.16 = bf16[8,40,128,18]{2,3,1,0:T(8,128)(2,1)} fusion(f32[128]{0:T(128)S(1)} %get-tuple-element.79, bf16[8,40,18,128]{3,1,2,0:T(8,128)(2,1)} %bitcast.654, bf16[4,18,128]{2,1,0:T(8,128)(2,1)} %copy-done.19, bf16[4,128,18]{1,2,0:T(8,128)(2,1)S(1)} %all_gather.26), kind=kOutput, calls=%fused_computation.48 | convolution fusion | flops 408944640 | bytes 2961920 | tf_op jit(solution)/shard_map/fh,xyhz->xyfz/dot_general | solution.py:134
  450.4 1.7 copy.625
  458.3 4.6 collective-permute-done.35
  464.7 13.8 %all_to_all.12 = bf16[4,1,8,40,2,128]{5,4,3,2,1,0:T(2,128)(2,1)S(1)} all-to-all(bf16[4,1,8,40,2,128]{5,4,3,2,1,0:T(2,128)(2,1)S(1)} %copy.365), channel_id=1, replica_groups=mesh['section'=4,'coil'=4,'cuts'=2] {'section'}, dimensions={0} | all-to-all | bytes 1310720 | tf_op jit(solution)/shard_map/all_to_all | solution.py:267
  (310 shorter events, 94.7 us)
Async XLA Ops:
  6.5 9.3 %copy-start = (bf16[2,1,32,80,2,128]{5,4,3,2,1,0:T(2,128)(2,1)S(1)}, bf16[2,1,32,80,2,128]{5,4,3,2,1,0:T(2,128)(2,1)}, u32[]{:S(2)}) copy-start(bf16[2,1,32,80,2,128]{5,4,3,2,1,0:T(2,128)(2,1)} %param.11) | copy-start | bytes 7864324
  6.5 99.6 %reduce-scatter.9.cloned.1.call-start = ((), (), s32[]{:S(2)}) async-start(), calls=%async_computation.9 | async-start | bytes 1638400 | tf_op jit(solution)/shard_map/reduce_scatter | solution.py:144
  9.9 22.5 %collective-permute-start.2 = (bf16[8,80,2,128]{3,1,2,0:T(8,128)(2,1)S(1)}, bf16[8,80,2,128]{3,1,2,0:T(8,128)(2,1)}, u32[]{:S(2)}, u32[]{:S(2)}) collective-permute-start(bf16[8,80,2,128]{3,1,2,0:T(8,128)(2,1)S(1)} %bitcast.658), channel_id=1, source_target_pairs={{0,6},{2,0},{4,2},{6,4},{1,7},{3,1},{5,3},{7,5},{8,14},{10,8},{12,... | collective-permute-start | bytes 983048 | tf_op jit(solution)/shard_map/ppermute | solution.py:168
  14.9 15.3 %collective-permute-start = (bf16[8,80,2,128]{3,1,2,0:T(8,128)(2,1)S(1)}, bf16[8,80,2,128]{3,1,2,0:T(8,128)(2,1)}, u32[]{:S(2)}, u32[]{:S(2)}) collective-permute-start(bf16[8,80,2,128]{3,1,2,0:T(8,128)(2,1)S(1)} %bitcast.659), channel_id=1, source_target_pairs={{0,2},{2,4},{4,6},{6,0},{1,3},{3,5},{5,7},{7,1},{8,10},{10,12},{12... | collective-permute-start | bytes 983048 | tf_op jit(solution)/shard_map/ppermute | solution.py:166
  30.2 10.9 %collective-permute-start.1 = (bf16[8,80,2,128]{3,1,2,0:T(8,128)(2,1)}, bf16[8,80,2,128]{3,1,2,0:T(8,128)(2,1)S(1)}, u32[]{:S(2)}, u32[]{:S(2)}) collective-permute-start(bf16[8,80,2,128]{3,1,2,0:T(8,128)(2,1)} %collective-permute-done), channel_id=1, source_target_pairs={{0,2},{2,4},{4,6},{6,0},{1,3},{3,5},{5,7},{7,1},{8,10},{10,12},{12... | collective-permute-start | bytes 983048 | tf_op jit(solution)/shard_map/ppermute | solution.py:166
  32.4 11.4 %copy-start.10 = (bf16[128,128]{1,0:T(8,128)(2,1)}, bf16[128,128]{1,0:T(8,128)(2,1)S(1)}, u32[]{:S(2)}) copy-start(bf16[128,128]{1,0:T(8,128)(2,1)S(1)} %get-tuple-element.92) | copy-start | bytes 98308
  44.8 8.1 %collective-permute-start.3 = (bf16[16,40,2,128]{3,1,0,2:T(8,128)(2,1)S(1)}, bf16[16,40,2,128]{3,1,0,2:T(8,128)(2,1)S(1)}, u32[]{:S(2)}, u32[]{:S(2)}) collective-permute-start(bf16[16,40,2,128]{3,1,0,2:T(8,128)(2,1)S(1)} %dynamic-slice_bitcast_fusion.7), channel_id=1, source_target_pairs={{0,8},{8,0},{16,24},{24,16},{1,9},{9,1},{17,25},{25,17},{2,10},{10... | collective-permute-start | bytes 983048 | tf_op jit(solution)/shard_map/ppermute | solution.py:28
  46.7 237.3 %copy-start.13 = (bf16[2,32,2,32,1]{1,3,0,4,2:T(8,128)(2,1)}, bf16[2,32,2,32,1]{1,3,0,4,2:T(8,128)(2,1)S(1)}, u32[]{:S(2)}) copy-start(bf16[2,32,2,32,1]{1,3,0,4,2:T(8,128)(2,1)S(1)} %copy.368) | copy-start | bytes 24580
  54.3 7.3 %collective-permute-start.4 = (bf16[16,40,2,128]{3,1,0,2:T(8,128)(2,1)S(1)}, bf16[16,40,2,128]{3,1,0,2:T(8,128)(2,1)S(1)}, u32[]{:S(2)}, u32[]{:S(2)}) collective-permute-start(bf16[16,40,2,128]{3,1,0,2:T(8,128)(2,1)S(1)} %dynamic-slice_bitcast_fusion.6), channel_id=1, source_target_pairs={{0,8},{8,0},{16,24},{24,16},{1,9},{9,1},{17,25},{25,17},{2,10},{10... | collective-permute-start | bytes 983048 | tf_op jit(solution)/shard_map/ppermute | solution.py:28
  56.3 238.0 %copy-start.15 = (bf16[128,128]{1,0:T(8,128)(2,1)}, bf16[128,128]{1,0:T(8,128)(2,1)S(1)}, u32[]{:S(2)}) copy-start(bf16[128,128]{1,0:T(8,128)(2,1)S(1)} %get-tuple-element.94) | copy-start | bytes 98308
  56.3 238.0 %copy-start.17 = (bf16[128,128]{1,0:T(8,128)(2,1)}, bf16[128,128]{1,0:T(8,128)(2,1)S(1)}, u32[]{:S(2)}) copy-start(bf16[128,128]{1,0:T(8,128)(2,1)S(1)} %get-tuple-element.95) | copy-start | bytes 98308
  64.6 14.4 %copy-start.24 = (bf16[1,128,18]{1,2,0:T(8,128)(2,1)S(1)}, bf16[1,128,18]{1,2,0:T(8,128)(2,1)}, u32[]{:S(2)}) copy-start(bf16[1,128,18]{1,2,0:T(8,128)(2,1)} %param.15) | copy-start | bytes 13828
  64.6 31.5 %copy-start.25 = (bf16[1,18,128]{2,1,0:T(8,128)(2,1)S(1)}, bf16[1,18,128]{2,1,0:T(8,128)(2,1)}, u32[]{:S(2)}) copy-start(bf16[1,18,128]{2,1,0:T(8,128)(2,1)} %param.17) | copy-start | bytes 13828
  65.8 58.7 %reduce-scatter.11.cloned.1.call-start = ((), (), s32[]{:S(2)}) async-start(), calls=%async_computation.10 | async-start | bytes 491520 | tf_op jit(solution)/shard_map/reduce_scatter | solution.py:150
  65.9 37.6 %collective-permute-start.6 = (bf16[8,1,2,128]{3,1,2,0:T(2,128)(2,1)S(1)}, bf16[8,1,2,128]{3,1,2,0:T(2,128)(2,1)S(1)}, u32[]{:S(2)}, u32[]{:S(2)}) collective-permute-start(bf16[8,1,2,128]{3,1,2,0:T(2,128)(2,1)S(1)} %get-tuple-element.70), channel_id=1, source_target_pairs={{0,1},{2,3},{4,5},{6,7},{8,9},{10,11},{12,13},{14,15},{16,17},{18,... | collective-permute-start | bytes 12296 | tf_op jit(solution)/shard_map/ppermute | solution.py:15
  67.2 36.3 %collective-permute-start.7 = (bf16[8,1,2,128]{3,1,2,0:T(2,128)(2,1)S(1)}, bf16[8,1,2,128]{3,1,2,0:T(2,128)(2,1)S(1)}, u32[]{:S(2)}, u32[]{:S(2)}) collective-permute-start(bf16[8,1,2,128]{3,1,2,0:T(2,128)(2,1)S(1)} %get-tuple-element.71), channel_id=1, source_target_pairs={{1,0},{3,2},{5,4},{7,6},{9,8},{11,10},{13,12},{15,14},{17,16},{19,... | collective-permute-start | bytes 12296 | tf_op jit(solution)/shard_map/ppermute | solution.py:16
  103.5 225.7 %copy-start.19 = (bf16[4,18,128]{2,1,0:T(8,128)(2,1)}, bf16[4,18,128]{2,1,0:T(8,128)(2,1)S(1)}, u32[]{:S(2)}) copy-start(bf16[4,18,128]{2,1,0:T(8,128)(2,1)S(1)} %all_gather.28) | copy-start | bytes 55300
  108.0 108.9 %reduce-scatter.13.cloned.1.call-start = ((), (), s32[]{:S(2)}) async-start(), calls=%async_computation.11 | async-start | bytes 1638400 | tf_op jit(solution)/shard_map/reduce_scatter | solution.py:144
  121.2 5.8 %collective-permute-start.8 = (bf16[8,1,18,128]{3,1,2,0:T(2,128)(2,1)S(1)}, bf16[8,1,18,128]{3,1,2,0:T(2,128)(2,1)S(1)}, u32[]{:S(2)}, u32[]{:S(2)}) collective-permute-start(bf16[8,1,18,128]{3,1,2,0:T(2,128)(2,1)S(1)} %get-tuple-element.20), channel_id=1, source_target_pairs={{0,1},{2,3},{4,5},{6,7},{8,9},{10,11},{12,13},{14,15},{16,17},{18,... | collective-permute-start | bytes 110600 | tf_op jit(solution)/shard_map/ppermute | solution.py:15
  122.5 4.5 collective-permute-start.9
  125.5 7.0 %collective-permute-start.5 = (bf16[8,40,2,128]{3,1,2,0:T(8,128)(2,1)S(1)}, bf16[8,40,2,128]{3,1,2,0:T(8,128)(2,1)S(1)}, u32[]{:S(2)}, u32[]{:S(2)}) collective-permute-start(bf16[8,40,2,128]{3,1,2,0:T(8,128)(2,1)S(1)} %copy.299), channel_id=1, source_target_pairs={{0,8},{8,0},{16,24},{24,16},{1,9},{9,1},{17,25},{25,17},{2,10},{10... | collective-permute-start | bytes 491528 | tf_op jit(solution)/shard_map/ppermute | solution.py:28
  135.8 12.4 %collective-permute-start.10 = (bf16[8,80,2,128]{3,1,2,0:T(8,128)(2,1)S(1)}, bf16[8,80,2,128]{3,1,2,0:T(8,128)(2,1)S(1)}, u32[]{:S(2)}, u32[]{:S(2)}) collective-permute-start(bf16[8,80,2,128]{3,1,2,0:T(8,128)(2,1)S(1)} %all_gather.29), channel_id=1, source_target_pairs={{0,2},{2,4},{4,6},{6,0},{1,3},{3,5},{5,7},{7,1},{8,10},{10,12},{12... | collective-permute-start | bytes 983048 | tf_op jit(solution)/shard_map/ppermute | solution.py:166
  135.8 16.8 %collective-permute-start.12 = (bf16[8,80,2,128]{3,1,2,0:T(8,128)(2,1)S(1)}, bf16[8,80,2,128]{3,1,2,0:T(8,128)(2,1)S(1)}, u32[]{:S(2)}, u32[]{:S(2)}) collective-permute-start(bf16[8,80,2,128]{3,1,2,0:T(8,128)(2,1)S(1)} %all_gather.29), channel_id=1, source_target_pairs={{0,6},{2,0},{4,2},{6,4},{1,7},{3,1},{5,3},{7,5},{8,14},{10,8},{12,... | collective-permute-start | bytes 983048 | tf_op jit(solution)/shard_map/ppermute | solution.py:168
  148.2 13.2 %collective-permute-start.11 = (bf16[8,80,2,128]{3,1,2,0:T(8,128)(2,1)S(1)}, bf16[8,80,2,128]{3,1,2,0:T(8,128)(2,1)S(1)}, u32[]{:S(2)}, u32[]{:S(2)}) collective-permute-start(bf16[8,80,2,128]{3,1,2,0:T(8,128)(2,1)S(1)} %collective-permute-done.10), channel_id=1, source_target_pairs={{0,2},{2,4},{4,6},{6,0},{1,3},{3,5},{5,7},{7,1},{8,10},{10,12},{12... | collective-permute-start | bytes 983048 | tf_op jit(solution)/shard_map/ppermute | solution.py:166
  164.4 9.0 %collective-permute-start.13 = (bf16[16,40,2,128]{3,1,0,2:T(8,128)(2,1)S(1)}, bf16[16,40,2,128]{3,1,0,2:T(8,128)(2,1)S(1)}, u32[]{:S(2)}, u32[]{:S(2)}) collective-permute-start(bf16[16,40,2,128]{3,1,0,2:T(8,128)(2,1)S(1)} %dynamic-slice_bitcast_fusion.5), channel_id=1, source_target_pairs={{0,8},{8,0},{16,24},{24,16},{1,9},{9,1},{17,25},{25,17},{2,10},{10... | collective-permute-start | bytes 983048 | tf_op jit(solution)/shard_map/ppermute | solution.py:28
  174.7 8.1 %collective-permute-start.14 = (bf16[16,40,2,128]{3,1,0,2:T(8,128)(2,1)S(1)}, bf16[16,40,2,128]{3,1,0,2:T(8,128)(2,1)S(1)}, u32[]{:S(2)}, u32[]{:S(2)}) collective-permute-start(bf16[16,40,2,128]{3,1,0,2:T(8,128)(2,1)S(1)} %dynamic-slice_bitcast_fusion.4), channel_id=1, source_target_pairs={{0,8},{8,0},{16,24},{24,16},{1,9},{9,1},{17,25},{25,17},{2,10},{10... | collective-permute-start | bytes 983048 | tf_op jit(solution)/shard_map/ppermute | solution.py:28
  187.0 48.1 %reduce-scatter.15.cloned.1.call-start = ((), (), s32[]{:S(2)}) async-start(), calls=%async_computation.12 | async-start | bytes 491520 | tf_op jit(solution)/shard_map/reduce_scatter | solution.py:150
  187.1 2.6 collective-permute-start.16
  188.4 3.1 collective-permute-start.17
  192.7 26.6 %copy-start.28 = (f32[128]{0:T(128)S(1)}, f32[128]{0:T(128)}, u32[]{:S(2)}) copy-start(f32[128]{0:T(128)} %get-tuple-element.78) | copy-start | bytes 1540
  218.7 108.3 %reduce-scatter.17.cloned.1.call-start = ((), (), s32[]{:S(2)}) async-start(), calls=%async_computation.13 | async-start | bytes 1638400 | tf_op jit(solution)/shard_map/reduce_scatter | solution.py:144
  232.4 5.2 %collective-permute-start.18 = (bf16[8,1,18,128]{3,1,2,0:T(2,128)(2,1)S(1)}, bf16[8,1,18,128]{3,1,2,0:T(2,128)(2,1)S(1)}, u32[]{:S(2)}, u32[]{:S(2)}) collective-permute-start(bf16[8,1,18,128]{3,1,2,0:T(2,128)(2,1)S(1)} %get-tuple-element.18), channel_id=1, source_target_pairs={{0,1},{2,3},{4,5},{6,7},{8,9},{10,11},{12,13},{14,15},{16,17},{18,... | collective-permute-start | bytes 110600 | tf_op jit(solution)/shard_map/ppermute | solution.py:15
  233.8 3.9 collective-permute-start.19
  236.1 7.0 %collective-permute-start.15 = (bf16[8,40,2,128]{3,1,2,0:T(8,128)(2,1)S(1)}, bf16[8,40,2,128]{3,1,2,0:T(8,128)(2,1)S(1)}, u32[]{:S(2)}, u32[]{:S(2)}) collective-permute-start(bf16[8,40,2,128]{3,1,2,0:T(8,128)(2,1)S(1)} %copy.319), channel_id=1, source_target_pairs={{0,8},{8,0},{16,24},{24,16},{1,9},{9,1},{17,25},{25,17},{2,10},{10... | collective-permute-start | bytes 491528 | tf_op jit(solution)/shard_map/ppermute | solution.py:28
  246.3 12.4 %collective-permute-start.20 = (bf16[8,80,2,128]{3,1,2,0:T(8,128)(2,1)S(1)}, bf16[8,80,2,128]{3,1,2,0:T(8,128)(2,1)S(1)}, u32[]{:S(2)}, u32[]{:S(2)}) collective-permute-start(bf16[8,80,2,128]{3,1,2,0:T(8,128)(2,1)S(1)} %all_gather.30), channel_id=1, source_target_pairs={{0,2},{2,4},{4,6},{6,0},{1,3},{3,5},{5,7},{7,1},{8,10},{10,12},{12... | collective-permute-start | bytes 983048 | tf_op jit(solution)/shard_map/ppermute | solution.py:166
  246.3 16.8 %collective-permute-start.22 = (bf16[8,80,2,128]{3,1,2,0:T(8,128)(2,1)S(1)}, bf16[8,80,2,128]{3,1,2,0:T(8,128)(2,1)S(1)}, u32[]{:S(2)}, u32[]{:S(2)}) collective-permute-start(bf16[8,80,2,128]{3,1,2,0:T(8,128)(2,1)S(1)} %all_gather.30), channel_id=1, source_target_pairs={{0,6},{2,0},{4,2},{6,4},{1,7},{3,1},{5,3},{7,5},{8,14},{10,8},{12,... | collective-permute-start | bytes 983048 | tf_op jit(solution)/shard_map/ppermute | solution.py:168
  258.8 13.2 %collective-permute-start.21 = (bf16[8,80,2,128]{3,1,2,0:T(8,128)(2,1)S(1)}, bf16[8,80,2,128]{3,1,2,0:T(8,128)(2,1)S(1)}, u32[]{:S(2)}, u32[]{:S(2)}) collective-permute-start(bf16[8,80,2,128]{3,1,2,0:T(8,128)(2,1)S(1)} %collective-permute-done.20), channel_id=1, source_target_pairs={{0,2},{2,4},{4,6},{6,0},{1,3},{3,5},{5,7},{7,1},{8,10},{10,12},{12... | collective-permute-start | bytes 983048 | tf_op jit(solution)/shard_map/ppermute | solution.py:166
  274.7 9.2 %copy-start.8 = (bf16[1,1,32,40,2,128]{5,4,3,2,1,0:T(2,128)(2,1)S(1)}, bf16[1,1,32,40,2,128]{5,4,3,2,1,0:T(2,128)(2,1)}, u32[]{:S(2)}) copy-start(bf16[1,1,32,40,2,128]{5,4,3,2,1,0:T(2,128)(2,1)} %copy-done.6) | copy-start | bytes 1966084
  274.7 9.2 %copy-start.22 = (f32[40,128]{1,0:T(8,128)S(1)}, f32[40,128]{1,0:T(8,128)}, u32[]{:S(2)}) copy-start(f32[40,128]{1,0:T(8,128)} %copy-done.20) | copy-start | bytes 61444
  274.8 9.0 %collective-permute-start.23 = (bf16[16,40,2,128]{3,1,0,2:T(8,128)(2,1)S(1)}, bf16[16,40,2,128]{3,1,0,2:T(8,128)(2,1)S(1)}, u32[]{:S(2)}, u32[]{:S(2)}) collective-permute-start(bf16[16,40,2,128]{3,1,0,2:T(8,128)(2,1)S(1)} %dynamic-slice_bitcast_fusion.3), channel_id=1, source_target_pairs={{0,8},{8,0},{16,24},{24,16},{1,9},{9,1},{17,25},{25,17},{2,10},{10... | collective-permute-start | bytes 983048 | tf_op jit(solution)/shard_map/ppermute | solution.py:28
  285.1 8.1 %collective-permute-start.24 = (bf16[16,40,2,128]{3,1,0,2:T(8,128)(2,1)S(1)}, bf16[16,40,2,128]{3,1,0,2:T(8,128)(2,1)S(1)}, u32[]{:S(2)}, u32[]{:S(2)}) collective-permute-start(bf16[16,40,2,128]{3,1,0,2:T(8,128)(2,1)S(1)} %dynamic-slice_bitcast_fusion.2), channel_id=1, source_target_pairs={{0,8},{8,0},{16,24},{24,16},{1,9},{9,1},{17,25},{25,17},{2,10},{10... | collective-permute-start | bytes 983048 | tf_op jit(solution)/shard_map/ppermute | solution.py:28
  297.4 47.7 %reduce-scatter.19.cloned.1.call-start = ((), (), s32[]{:S(2)}) async-start(), calls=%async_computation.14 | async-start | bytes 491520 | tf_op jit(solution)/shard_map/reduce_scatter | solution.py:150
  297.5 2.6 collective-permute-start.26
  298.8 3.1 collective-permute-start.27
  303.1 26.1 %copy-start.27 = (f32[128]{0:T(128)S(1)}, f32[128]{0:T(128)}, u32[]{:S(2)}) copy-start(f32[128]{0:T(128)} %get-tuple-element.77) | copy-start | bytes 1540
  328.9 108.3 %reduce-scatter.21.cloned.1.call-start = ((), (), s32[]{:S(2)}) async-start(), calls=%async_computation.15 | async-start | bytes 1638400 | tf_op jit(solution)/shard_map/reduce_scatter | solution.py:144
  342.4 5.2 %collective-permute-start.28 = (bf16[8,1,18,128]{3,1,2,0:T(2,128)(2,1)S(1)}, bf16[8,1,18,128]{3,1,2,0:T(2,128)(2,1)S(1)}, u32[]{:S(2)}, u32[]{:S(2)}) collective-permute-start(bf16[8,1,18,128]{3,1,2,0:T(2,128)(2,1)S(1)} %get-tuple-element.16), channel_id=1, source_target_pairs={{0,1},{2,3},{4,5},{6,7},{8,9},{10,11},{12,13},{14,15},{16,17},{18,... | collective-permute-start | bytes 110600 | tf_op jit(solution)/shard_map/ppermute | solution.py:15
  343.8 3.8 collective-permute-start.29
  346.1 7.0 %collective-permute-start.25 = (bf16[8,40,2,128]{3,1,2,0:T(8,128)(2,1)S(1)}, bf16[8,40,2,128]{3,1,2,0:T(8,128)(2,1)S(1)}, u32[]{:S(2)}, u32[]{:S(2)}) collective-permute-start(bf16[8,40,2,128]{3,1,2,0:T(8,128)(2,1)S(1)} %copy.339), channel_id=1, source_target_pairs={{0,8},{8,0},{16,24},{24,16},{1,9},{9,1},{17,25},{25,17},{2,10},{10... | collective-permute-start | bytes 491528 | tf_op jit(solution)/shard_map/ppermute | solution.py:28
  356.3 12.4 %collective-permute-start.30 = (bf16[8,80,2,128]{3,1,2,0:T(8,128)(2,1)S(1)}, bf16[8,80,2,128]{3,1,2,0:T(8,128)(2,1)S(1)}, u32[]{:S(2)}, u32[]{:S(2)}) collective-permute-start(bf16[8,80,2,128]{3,1,2,0:T(8,128)(2,1)S(1)} %all_gather.31), channel_id=1, source_target_pairs={{0,2},{2,4},{4,6},{6,0},{1,3},{3,5},{5,7},{7,1},{8,10},{10,12},{12... | collective-permute-start | bytes 983048 | tf_op jit(solution)/shard_map/ppermute | solution.py:166
  356.3 16.8 %collective-permute-start.32 = (bf16[8,80,2,128]{3,1,2,0:T(8,128)(2,1)S(1)}, bf16[8,80,2,128]{3,1,2,0:T(8,128)(2,1)S(1)}, u32[]{:S(2)}, u32[]{:S(2)}) collective-permute-start(bf16[8,80,2,128]{3,1,2,0:T(8,128)(2,1)S(1)} %all_gather.31), channel_id=1, source_target_pairs={{0,6},{2,0},{4,2},{6,4},{1,7},{3,1},{5,3},{7,5},{8,14},{10,8},{12,... | collective-permute-start | bytes 983048 | tf_op jit(solution)/shard_map/ppermute | solution.py:168
  368.7 13.2 %collective-permute-start.31 = (bf16[8,80,2,128]{3,1,2,0:T(8,128)(2,1)S(1)}, bf16[8,80,2,128]{3,1,2,0:T(8,128)(2,1)S(1)}, u32[]{:S(2)}, u32[]{:S(2)}) collective-permute-start(bf16[8,80,2,128]{3,1,2,0:T(8,128)(2,1)S(1)} %collective-permute-done.30), channel_id=1, source_target_pairs={{0,2},{2,4},{4,6},{6,0},{1,3},{3,5},{5,7},{7,1},{8,10},{10,12},{12... | collective-permute-start | bytes 983048 | tf_op jit(solution)/shard_map/ppermute | solution.py:166
  384.8 9.2 %copy-start.9 = (bf16[1,1,32,40,2,128]{5,4,3,2,1,0:T(2,128)(2,1)S(1)}, bf16[1,1,32,40,2,128]{5,4,3,2,1,0:T(2,128)(2,1)}, u32[]{:S(2)}) copy-start(bf16[1,1,32,40,2,128]{5,4,3,2,1,0:T(2,128)(2,1)} %copy-done.6) | copy-start | bytes 1966084
  384.8 9.2 %copy-start.14 = (bf16[2,32,2,32,1]{1,3,0,4,2:T(8,128)(2,1)S(1)}, bf16[2,32,2,32,1]{1,3,0,4,2:T(8,128)(2,1)}, u32[]{:S(2)}) copy-start(bf16[2,32,2,32,1]{1,3,0,4,2:T(8,128)(2,1)} %copy-done.13) | copy-start | bytes 24580
  384.8 9.2 %copy-start.23 = (f32[40,128]{1,0:T(8,128)S(1)}, f32[40,128]{1,0:T(8,128)}, u32[]{:S(2)}) copy-start(f32[40,128]{1,0:T(8,128)} %copy-done.20) | copy-start | bytes 61444
  384.9 9.0 %collective-permute-start.33 = (bf16[16,40,2,128]{3,1,0,2:T(8,128)(2,1)S(1)}, bf16[16,40,2,128]{3,1,0,2:T(8,128)(2,1)S(1)}, u32[]{:S(2)}, u32[]{:S(2)}) collective-permute-start(bf16[16,40,2,128]{3,1,0,2:T(8,128)(2,1)S(1)} %dynamic-slice_bitcast_fusion.1), channel_id=1, source_target_pairs={{0,8},{8,0},{16,24},{24,16},{1,9},{9,1},{17,25},{25,17},{2,10},{10... | collective-permute-start | bytes 983048 | tf_op jit(solution)/shard_map/ppermute | solution.py:28
  395.2 8.1 %collective-permute-start.34 = (bf16[16,40,2,128]{3,1,0,2:T(8,128)(2,1)S(1)}, bf16[16,40,2,128]{3,1,0,2:T(8,128)(2,1)S(1)}, u32[]{:S(2)}, u32[]{:S(2)}) collective-permute-start(bf16[16,40,2,128]{3,1,0,2:T(8,128)(2,1)S(1)} %dynamic-slice_bitcast_fusion), channel_id=1, source_target_pairs={{0,8},{8,0},{16,24},{24,16},{1,9},{9,1},{17,25},{25,17},{2,10},{10... | collective-permute-start | bytes 983048 | tf_op jit(solution)/shard_map/ppermute | solution.py:28
  407.6 47.3 %reduce-scatter.23.cloned.1.call-start = ((), (), s32[]{:S(2)}) async-start(), calls=%async_computation.16 | async-start | bytes 491520 | tf_op jit(solution)/shard_map/reduce_scatter | solution.py:150
  407.7 2.9 collective-permute-start.36
  409.0 3.1 collective-permute-start.37
  452.3 5.2 %collective-permute-start.38 = (bf16[8,1,18,128]{3,1,2,0:T(2,128)(2,1)S(1)}, bf16[8,1,18,128]{3,1,2,0:T(2,128)(2,1)S(1)}, u32[]{:S(2)}, u32[]{:S(2)}) collective-permute-start(bf16[8,1,18,128]{3,1,2,0:T(2,128)(2,1)S(1)} %get-tuple-element.14), channel_id=1, source_target_pairs={{0,1},{2,3},{4,5},{6,7},{8,9},{10,11},{12,13},{14,15},{16,17},{18,... | collective-permute-start | bytes 110600 | tf_op jit(solution)/shard_map/ppermute | solution.py:15
  453.6 3.8 collective-permute-start.39
  455.9 7.0 %collective-permute-start.35 = (bf16[8,40,2,128]{3,1,2,0:T(8,128)(2,1)S(1)}, bf16[8,40,2,128]{3,1,2,0:T(8,128)(2,1)S(1)}, u32[]{:S(2)}, u32[]{:S(2)}) collective-permute-start(bf16[8,40,2,128]{3,1,2,0:T(8,128)(2,1)S(1)} %copy.359), channel_id=1, source_target_pairs={{0,8},{8,0},{16,24},{24,16},{1,9},{9,1},{17,25},{25,17},{2,10},{10... | collective-permute-start | bytes 491528 | tf_op jit(solution)/shard_map/ppermute | solution.py:28
  464.1 15.3 %copy-start.1 = (bf16[2,1,32,80,2,128]{5,4,3,2,1,0:T(2,128)(2,1)S(1)}, bf16[2,1,32,80,2,128]{5,4,3,2,1,0:T(2,128)(2,1)}, u32[]{:S(2)}) copy-start(bf16[2,1,32,80,2,128]{5,4,3,2,1,0:T(2,128)(2,1)} %param.11) | copy-start | bytes 7864324
  (14 other events, 70.5 us)
Sparse Core Ops, SparseCore 0:
  65.9 29.5 reduce-scatter.8
  108.1 4.9 reduce-scatter.10
  187.1 29.7 reduce-scatter.12
  219.0 6.4 reduce-scatter.14
  297.5 29.4 reduce-scatter.16
  329.2 6.4 reduce-scatter.18
  407.7 29.4 reduce-scatter.20
  439.5 6.4 reduce-scatter.22
